TPU v7x, 512 devices: a whole 4x4x16 slice. The times are simulated.
512 devices in a mesh: rows: 128 (over z, y, core), sub: 4 (over x).
Axes of the slice: x: 4, y: 4, z: 16, core: 2. Of those that a mesh axis runs over, the one named last changes fastest.
Arguments:
- factor_a: float32 [131072, 256], P(('rows', 'sub')), may hold values from -6 to 6
- factor_b: float32 [131072, 256], P(('rows', 'sub')), may hold values from -0.0009765625 to 0.0009765625
- value_diffs: float32 [131072, 32], P(('rows', 'sub')), may hold values from -6 to 6
- residual_diffs: float32 [131072, 32], P(('rows', 'sub')), may hold values from -6 to 6
- residual: float32 [131072], P(('rows', 'sub')), may hold values from -6 to 6
Outputs:
- update: float32 [131072], P(('rows', 'sub'))
- new_a: float32 [131072, 256], P(('rows', 'sub'))
- new_b: float32 [131072, 256], P(('rows', 'sub'))
All inputs are finite; a program needn't handle non-finite values.
Results may differ from a plain program's by a relative error of at most 0.0003.
Values sent between devices are 32-bit elements; how exact they have to be, the bound alone decides.
A program may use at most 64 MiB of HBM per device.

v0:
```python
import jax
import jax.numpy as jnp
from jax import lax
from jax.sharding import PartitionSpec as P


def matmul(left, right):
    return jnp.dot(left, right, precision=lax.Precision.HIGHEST, preferred_element_type=jnp.float32)


def small_inverse(lower):
    extent = lower.shape[0]
    diag_inv = 1.0 / jnp.diagonal(lower)
    strict = jnp.tril(lower, -1) * diag_inv[:, None]
    ident = jnp.eye(extent, dtype=lower.dtype)
    result = ident - strict
    power = strict
    for level in range(3):
        power = matmul(power, power)
        result = matmul(result, ident + power)
    return result * diag_inv[None, :]


def lower_inverse(lower):
    extent = lower.shape[0]
    if extent <= 8:
        return small_inverse(lower)
    half = extent // 2
    upper_inv = lower_inverse(lower[:half, :half])
    tail_inv = lower_inverse(lower[half:, half:])
    corner = -matmul(tail_inv, matmul(lower[half:, :half], upper_inv))
    zeros = jnp.zeros((half, extent - half), lower.dtype)
    return jnp.concatenate(
        [jnp.concatenate([upper_inv, zeros], axis=1), jnp.concatenate([corner, tail_inv], axis=1)],
        axis=0,
    )


def tri_solve(matrix, rhs, lower):
    if lower:
        return matmul(lower_inverse(matrix), rhs)
    return matmul(lower_inverse(matrix.T).T, rhs)


def inverse_gram(gram_v):
    low_v = jnp.linalg.cholesky(gram_v)
    low_inv = lower_inverse(low_v)
    return matmul(low_inv.T, low_inv)


def truncate(gram_a, gram_b, width):
    low_a = jnp.linalg.cholesky(gram_a)
    low_b = jnp.linalg.cholesky(gram_b)
    core = matmul(low_a.T, low_b)
    start = matmul(core.T, core[:, :width])
    low_y = jnp.linalg.cholesky(matmul(start.T, start))
    basis = tri_solve(low_y, start.T, True).T
    return (matmul(low_b, basis), tri_solve(low_b.T, basis, False))


def on_device(factor_a, factor_b, value_diffs, residual_diffs, residual):
    width = factor_a.shape[1]
    gram_v = matmul(residual_diffs.T, residual_diffs)
    proj = matmul(factor_b.T, residual_diffs)
    proj_r = matmul(factor_b.T, residual)
    gram_r = matmul(residual_diffs.T, residual)
    sent_v = gram_v
    sent_v, proj, proj_r, gram_r = lax.psum((sent_v, proj, proj_r, gram_r), ("rows", "sub"))
    gram_v = sent_v
    inv_v = inverse_gram(gram_v)
    fresh = value_diffs - matmul(factor_a, proj)
    scaled_v = matmul(residual_diffs, inv_v)
    wide_a = jnp.concatenate([factor_a, fresh], axis=1)
    wide_b = jnp.concatenate([factor_b, scaled_v], axis=1)
    gram_a = matmul(wide_a.T, wide_a)
    gram_b = matmul(wide_b.T, wide_b)
    sent_a = gram_a
    sent_b = gram_b
    sent_a, sent_b = lax.psum((sent_a, sent_b), ("rows", "sub"))
    gram_a = sent_a
    gram_b = sent_b
    coeffs = -matmul(inv_v, gram_r)
    update = -matmul(factor_a, proj_r) + matmul(fresh, coeffs)
    left_map, right_map = truncate(gram_a, gram_b, width)
    return (update, matmul(wide_a, left_map), matmul(wide_b, right_map))


def solution(mesh):
    placed = (
        P(("rows", "sub"), None),
        P(("rows", "sub"), None),
        P(("rows", "sub"), None),
        P(("rows", "sub"), None),
        P(("rows", "sub")),
    )
    return jax.shard_map(
        on_device,
        mesh=mesh,
        in_specs=placed,
        out_specs=(P(("rows", "sub")), P(("rows", "sub"), None), P(("rows", "sub"), None)),
        check_vma=False,
    )
```

profile of v0, /device:TPU:1, one launch (start us, length us, event | category | flops | bytes accessed | tf_op | source)
XLA Modules:
  0.0 957.2 jit_solution(16427618068768078991)
XLA Ops:
  7.2 0.7 copy-done
  8.1 1.5 fusion.2054
  9.7 0.7 copy-done.7
  10.7 111.9 %all-reduce.99 = (f32[256,32]{1,0:T(8,128)S(1)}, f32[32,32]{0,1:T(8,128)S(1)}, f32[32]{0:T(128)S(1)}, f32[256]{0:T(256)S(1)}) all-reduce(f32[256,32]{1,0:T(8,128)S(1)} %fusion.2054, f32[32,32]{0,1:T(8,128)S(1)} %fusion.2055, f32[32]{0:T(128)S(1)} %convolution_bitcast_fusion.2, ...), channel_id=1, replica_groups=mesh['rows'=128,'sub'=4] {'rows','sub'}, use_global_device_ids=true, to_apply=%region_1.0 | all-reduce | flops 9504 | bytes 76032 | tf_op jit(solution)/shard_map/psum | solution.py:68
  122.7 2.9 cholesky.201
  135.2 1.7 fusion.34
  137.3 1.7 fusion.36
  140.3 460.4 %all-reduce.103.cloned.1.call-done = (f32[288,288]{0,1:T(8,128)}, f32[288,288]{0,1:T(8,128)}) async-done(((f32[288,288]{0,1:T(8,128)}, f32[288,288]{0,1:T(8,128)}), (f32[288,288]{0,1:T(8,128)}, f32[288,288]{0,1:T(8,128)})) %all-reduce.103.cloned.1.call-update) | async-done | bytes 663568 | tf_op jit(solution)/shard_map/psum | solution.py:79
  600.7 1.3 copy.58
  602.2 0.8 copy-done.4
  603.2 0.8 copy-done.5
  603.9 11.7 %cholesky.370 = f32[128,128]{1,0:T(8,128)S(1)} custom-call(f32[128,128]{1,0:T(8,128)S(1)} %cholesky.480), custom_call_target="Cholesky" | custom-call | tf_op jit(solution)/shard_map/jit(cholesky)/cholesky | solution.py:53
  615.7 11.7 %cholesky.427 = f32[128,128]{1,0:T(8,128)S(1)} custom-call(f32[128,128]{1,0:T(8,128)S(1)} %cholesky.488), custom_call_target="Cholesky" | custom-call | tf_op jit(solution)/shard_map/jit(cholesky)/cholesky | solution.py:52
  627.5 10.0 %custom-call.231 = f32[1,128,128]{1,2,0:T(8,128)S(1)} custom-call(f32[1,128,128]{2,1,0:T(8,128)S(1)} %get-tuple-element.119), custom_call_target="InvertDiagBlocksLowerTriangular" | custom-call | tf_op jit(solution)/shard_map/jit(cholesky)/cholesky | solution.py:53
  637.5 1.1 constant_dynamic-update-slice_fusion.3
  638.6 1.2 convolution_subtract_fusion.1
  639.8 11.7 %cholesky.389 = f32[128,128]{1,0:T(8,128)S(1)} custom-call(f32[128,128]{1,0:T(8,128)S(1)} %cholesky.484), custom_call_target="Cholesky" | custom-call | tf_op jit(solution)/shard_map/jit(cholesky)/cholesky | solution.py:53
  651.5 9.8 %custom-call.232 = f32[1,128,128]{1,2,0:T(8,128)S(1)} custom-call(f32[1,128,128]{2,1,0:T(8,128)S(1)} %get-tuple-element.116), custom_call_target="InvertDiagBlocksLowerTriangular" | custom-call | tf_op jit(solution)/shard_map/jit(cholesky)/cholesky | solution.py:53
  661.5 0.9 convolution_subtract_fusion.4
  662.4 2.9 cholesky.411
  666.6 0.7 compare_reduce_fusion.3
  667.3 9.8 %custom-call.233 = f32[1,128,128]{1,2,0:T(8,128)S(1)} custom-call(f32[1,128,128]{2,1,0:T(8,128)S(1)} %get-tuple-element.114), custom_call_target="InvertDiagBlocksLowerTriangular" | custom-call | tf_op jit(solution)/shard_map/jit(cholesky)/cholesky | solution.py:52
  677.6 11.9 %cholesky.446 = f32[128,128]{1,0:T(8,128)S(1)} custom-call(f32[128,128]{1,0:T(8,128)S(1)} %cholesky.492), custom_call_target="Cholesky" | custom-call | tf_op jit(solution)/shard_map/jit(cholesky)/cholesky | solution.py:52
  689.6 9.8 %custom-call.234 = f32[1,128,128]{1,2,0:T(8,128)S(1)} custom-call(f32[1,128,128]{2,1,0:T(8,128)S(1)} %get-tuple-element.111), custom_call_target="InvertDiagBlocksLowerTriangular" | custom-call | tf_op jit(solution)/shard_map/jit(cholesky)/cholesky | solution.py:52
  699.7 2.9 cholesky.468
  704.0 0.7 compare_reduce_fusion
  708.5 1.0 fusion.30
  709.6 1.1 fusion.37
  710.7 0.8 fusion.2061
  711.7 12.1 %cholesky.218 = f32[128,128]{1,0:T(8,128)S(1)} custom-call(f32[128,128]{1,0:T(8,128)S(1)} %cholesky.496), custom_call_target="Cholesky" | custom-call | tf_op jit(solution)/shard_map/jit(cholesky)/cholesky | solution.py:56
  723.8 9.8 %custom-call.28 = f32[1,128,128]{1,2,0:T(8,128)S(1)} custom-call(f32[1,128,128]{2,1,0:T(8,128)S(1)} %get-tuple-element.109), custom_call_target="InvertDiagBlocksLowerTriangular" | custom-call | tf_op jit(solution)/shard_map/jit(cholesky)/cholesky | solution.py:56
  734.1 11.7 %cholesky.284 = f32[128,128]{1,0:T(8,128)S(1)} custom-call(f32[128,128]{1,0:T(8,128)S(1)} %convolution_subtract_fusion.2), custom_call_target="Cholesky" | custom-call | tf_op jit(solution)/shard_map/jit(cholesky)/cholesky | solution.py:56
  810.3 0.7 gather_fusion.38
  813.4 0.7 gather_fusion.42
  820.3 0.7 gather_fusion.50
  829.7 0.7 gather_fusion.46
  844.9 0.7 gather_fusion.62
  852.9 0.7 gather_fusion.54
  855.9 0.7 gather_fusion.58
  866.7 0.7 gather_fusion.98
  876.1 0.7 gather_fusion.94
  884.1 0.7 gather_fusion.86
  886.0 0.9 gather_fusion.91
  887.4 0.7 gather_fusion.90
  900.6 0.7 gather_fusion.70
  937.4 1.3 fusion.35
  947.6 1.1 fusion.3
  948.7 1.3 fusion.33
  (1156 shorter events, 205.8 us)
Async XLA Ops:
  7.2 0.8 copy-start
  7.2 3.3 copy-start.2
  7.2 593.5 %all-reduce.103.cloned.1.call-start = ((), (), s32[]{:S(2)}) async-start(), calls=%async_computation | async-start | bytes 1769472 | tf_op jit(solution)/shard_map/psum | solution.py:79
  9.6 0.7 copy-start.7
  135.2 1.7 copy-start.1
  135.2 1.7 copy-start.6
  600.7 1.3 copy-start.3
  602.0 1.0 copy-start.4
  603.2 0.8 copy-start.5
Sparse Core Ops, SparseCore 0:
  139.2 461.5 all-reduce.102
where the time goes:
time: 967 us; the launch traced here: 957 us
  waiting for transfers between devices  460 us (48%)
  matrix products  151 us (16%)
  other arithmetic  141 us (15%)
  blocking collectives  112 us (12%)
  local copies, waits for them, and re-layouts  71.2 us (7%)
  between operations  21.2 us (2%)
    psum x1, waiting for transfers between devices, on_device(): sent_a, sent_b = lax.psum((sent_a, sent_b), ('rows', 'sub'))  460 us
    dot_general x814, matrix products, matmul(): jnp.dot(left, right, precision=lax.Precision.HIGHEST, preferred_element_t...  147 us
    psum x1, blocking collectives, on_device(): lax.psum((sent_v, proj, proj_r, gram_r), ('rows', 'sub'))  112 us
    gather x100, local copies, waits for them, and re-layouts, small_inverse(): diag_inv = 1.0 / jnp.diagonal(lower)  65.3 us
    another operation x11, other arithmetic, truncate(): low_a = jnp.linalg.cholesky(gram_a)  48.2 us
    another operation x11, other arithmetic, truncate(): low_b = jnp.linalg.cholesky(gram_b)  48.2 us
    another operation x7, other arithmetic, truncate(): low_y = jnp.linalg.cholesky(matmul(start.T, start))  35 us
  transfers between devices with their start and end apart: 1, of which 1 were waited for; matrix products, arithmetic and copies ran while one was open for 0% of the time, Pallas kernels for 0%

commit v1 on v0

v1 whole, which is shorter than its diff:
```python
import functools

import jax
import jax.numpy as jnp
from jax import lax
from jax.experimental import pallas as pl
from jax.experimental.pallas import tpu as pltpu
from jax.sharding import PartitionSpec as P

MESH = pl.DeviceIdType.MESH
LANES = 128
PACK = 768
BLOCK = 32

NN = (((1,), (0,)), ((), ()))
NT = (((1,), (1,)), ((), ()))
TN = (((0,), (0,)), ((), ()))


def dot(left, right, dims=NN):
    return lax.dot_general(left, right, dims, precision=lax.Precision.HIGHEST, preferred_element_type=jnp.float32)


def pack_pair(gram, out_ref, base):
    row = lax.broadcasted_iota(jnp.int32, (LANES, LANES), 0)
    lane = lax.broadcasted_iota(jnp.int32, (LANES, LANES), 1)
    first, last = gram[:LANES, :LANES], gram[LANES:, LANES:]
    out_ref[base:base + LANES, :] = jnp.where(row >= lane, first, last)
    out_ref[base + LANES:base + 2 * LANES, :] = gram[LANES:, :LANES]
    return jnp.sum(jnp.where(row == lane, last, 0.0), axis=0, keepdims=True)


def unpack_pair(red_ref, base, diag):
    row = lax.broadcasted_iota(jnp.int32, (LANES, LANES), 0)
    lane = lax.broadcasted_iota(jnp.int32, (LANES, LANES), 1)
    both = red_ref[base:base + LANES, :]
    turned = both.T
    low = red_ref[base + LANES:base + 2 * LANES, :]
    first = jnp.where(row >= lane, both, turned)
    last = jnp.where(row < lane, both, jnp.where(row > lane, turned, diag))
    return jnp.concatenate(
        [jnp.concatenate([first, low.T], axis=1), jnp.concatenate([low, last], axis=1)], axis=0
    )


def reduce_kernel(sizes, a_ref, b_ref, v_ref, d_ref, r_ref, out_ref, local, pair, half, near, mine, far, total, full,
                  pair_sem, near_sem, far_sem, total_sem, back_sem, cross_sem,
                  pair_out, near_out, far_out, total_out, back_out, cross_out):
    nz, ny, nx = sizes
    peers = ny * nx
    rows = PACK // 2
    piece = rows // peers
    tiles = piece // 8
    place = lax.axis_index("rows")
    x = lax.axis_index("sub")
    core = lax.rem(place, 2)
    y = lax.rem(place // 2, ny)
    z = place // (2 * ny)
    me = y * nx + x
    near_ids = []
    for dy in range(ny):
        for dx in range(nx):
            if dy or dx:
                qy, qx = lax.rem(y + dy, ny), lax.rem(x + dx, nx)
                hops = min(dy, ny - dy) + min(dx, nx - dx)
                near_ids.append((hops, dy * nx + dx, qy * nx + qx, ((z * ny + qy) * 2 + core, qx)))
    near_ids = [item[2:] for item in sorted(near_ids, key=lambda item: (-item[0], item[1]))]
    far_ids = []
    for dz in sorted(range(1, nz), key=lambda d: -min(d, nz - d)):
        qz = lax.rem(z + dz, nz)
        far_ids.append((dz, qz, ((qz * ny + y) * 2 + core, x)))
    partner = (place + 1 - 2 * core, x)
    owners = [(t * nz) // tiles if nz >= tiles else t % nz for t in range(tiles)]

    barrier = pltpu.get_barrier_semaphore()
    for _, _, dev in far_ids:
        pl.semaphore_signal(barrier, inc=1, device_id=dev, device_id_type=MESH)
    for _, dev in near_ids:
        pl.semaphore_signal(barrier, inc=1, device_id=dev, device_id_type=MESH)
    pl.semaphore_signal(barrier, inc=1, device_id=partner, device_id_type=MESH)

    a, b = a_ref[...], b_ref[...]
    v, d = v_ref[...], d_ref[...]
    cols = v.shape[1]
    diag_a = pack_pair(dot(a, a, TN), local, 0)
    diag_b = pack_pair(dot(b, b, TN), local, 2 * LANES)
    va = dot(v, a, TN)
    left = jnp.concatenate([d.T, jnp.broadcast_to(r_ref[...], (8, d.shape[0]))], axis=0)
    db = dot(left, b)
    dd = dot(left, d)
    vv = dot(v, v, TN)
    local[512:512 + cols, :] = va[:, :LANES]
    local[512 + cols:576, :] = va[:, LANES:]
    local[576:616, :] = db[:, :LANES]
    local[616:656, :] = db[:, LANES:]
    local[656:696, :] = jnp.zeros((40, LANES), jnp.float32)
    local[656:656 + cols, 0:cols] = vv
    local[656:696, 64:64 + cols] = dd
    local[696:768, :] = jnp.zeros((72, LANES), jnp.float32)
    local[696:697, :] = diag_a
    local[697:698, :] = diag_b

    pl.semaphore_wait(barrier, len(far_ids) + len(near_ids) + 1)

    def send(src, dst, out_sem, in_sem, dev):
        copy = pltpu.make_async_remote_copy(
            src_ref=src, dst_ref=dst, send_sem=out_sem, recv_sem=in_sem, device_id=dev, device_id_type=MESH
        )
        copy.start()
        return copy

    def arrived(ref, sem):
        pltpu.make_async_copy(ref, ref, sem).wait()

    pending = []

    def ds(start, size):
        return pl.ds(pl.multiple_of(start, 8), size)

    pending.append(send(local.at[ds((1 - core) * rows, rows)], pair, pair_out, pair_sem, partner))
    arrived(pair, pair_sem)
    half[...] = local[ds(core * rows, rows), :] + pair[...]

    for k, (q, dev) in enumerate(near_ids):
        pending.append(send(half.at[ds(q * piece, piece)], near.at[me], near_out.at[k], near_sem.at[me], dev))
    value = half[ds(me * piece, piece), :]
    for q, _ in near_ids:
        arrived(near.at[q], near_sem.at[q])
        value = value + near[q]
    mine[...] = value

    for t, owner in enumerate(owners):
        tile = pl.ds(8 * t, 8)

        @pl.when(z != owner)
        def _():
            send(mine.at[tile], far.at[t, z], far_out.at[t], far_sem.at[t, z], ((owner * ny + y) * 2 + core, x))

    for t, owner in enumerate(owners):
        tile = pl.ds(8 * t, 8)

        @pl.when(z == owner)
        def _():
            value = mine[8 * t:8 * t + 8, :]
            for dz, qz, dev in far_ids:
                arrived(far.at[t, qz], far_sem.at[t, qz])
                value = value + far[t, qz]
            total[8 * t:8 * t + 8, :] = value
            for dz, qz, dev in far_ids:
                send(total.at[tile], total.at[tile], total_out.at[t, dz], total_sem.at[t], dev)

    for t, owner in enumerate(owners):
        tile = pl.ds(8 * t, 8)

        @pl.when(z != owner)
        def _():
            arrived(total.at[tile], total_sem.at[t])

    slot = core * peers
    for k, (q, dev) in enumerate(near_ids):
        pending.append(send(total, full.at[slot + me], back_out.at[k], back_sem.at[me], dev))
    pending.append(send(total, full.at[slot + me], cross_out.at[me], cross_sem.at[me], partner))
    full[slot + me] = total[...]
    for q, _ in reversed(near_ids):
        arrived(full.at[slot + q], back_sem.at[q])
        pending.append(send(full.at[slot + q], full.at[slot + q], cross_out.at[q], cross_sem.at[q], partner))
    other = (1 - core) * peers
    for q in range(peers):
        arrived(full.at[other + q], cross_sem.at[q])
    for q in range(2 * peers):
        out_ref[q * piece:(q + 1) * piece, :] = full[q]

    for copy in pending:
        copy.wait_send()
    for t, owner in enumerate(owners):
        tile = pl.ds(8 * t, 8)

        @pl.when(z != owner)
        def _():
            arrived(mine.at[tile], far_out.at[t])

        @pl.when(z == owner)
        def _():
            for dz, _, _ in far_ids:
                arrived(total.at[tile], total_out.at[t, dz])


def reduce_all(sizes, a, b, v, d, r):
    nz, ny, nx = sizes
    peers = ny * nx
    piece = PACK // 2 // peers
    tiles = piece // 8
    vmem = pl.BlockSpec(memory_space=pltpu.VMEM)
    dma = pltpu.SemaphoreType.DMA
    return pl.pallas_call(
        functools.partial(reduce_kernel, sizes),
        out_shape=jax.ShapeDtypeStruct((PACK, LANES), jnp.float32),
        in_specs=[vmem] * 5,
        out_specs=vmem,
        scratch_shapes=[
            pltpu.VMEM((PACK, LANES), jnp.float32),
            pltpu.VMEM((PACK // 2, LANES), jnp.float32),
            pltpu.VMEM((PACK // 2, LANES), jnp.float32),
            pltpu.VMEM((peers, piece, LANES), jnp.float32),
            pltpu.VMEM((piece, LANES), jnp.float32),
            pltpu.VMEM((tiles, nz, 8, LANES), jnp.float32),
            pltpu.VMEM((piece, LANES), jnp.float32),
            pltpu.VMEM((2 * peers, piece, LANES), jnp.float32),
            dma(()), dma((peers,)), dma((tiles, nz)), dma((tiles,)), dma((peers,)), dma((peers,)),
            dma(()), dma((peers,)), dma((tiles,)), dma((tiles, nz)), dma((peers,)), dma((peers,)),
        ],
        compiler_params=pltpu.CompilerParams(collective_id=0, has_side_effects=True, vmem_limit_bytes=32 << 20),
    )(a, b, v, d, r)


def eliminate(block):
    row = lax.broadcasted_iota(jnp.int32, (BLOCK, LANES), 0)
    for j in range(BLOCK):
        scale = lax.rsqrt(block[j:j + 1, j:j + 1])
        pivot = block[j:j + 1, :] * scale
        column = block[:, j:j + 1] * scale
        block = jnp.where(row > j, block - column * pivot, jnp.where(row == j, pivot, block))
    return pltpu.roll(block, LANES - BLOCK, 1)[:, :BLOCK]


def with_identity(block, offset):
    row = lax.broadcasted_iota(jnp.int32, (BLOCK, LANES), 0)
    lane = lax.broadcasted_iota(jnp.int32, (BLOCK, LANES), 1)
    if offset:
        block = pltpu.roll(block, LANES - offset, 1)
    return jnp.where(lane < BLOCK, block, jnp.where(lane == row + BLOCK, 1.0, 0.0))


def largest(values):
    return jnp.max(jnp.max(values, axis=1, keepdims=True), axis=0, keepdims=True)


def diagonal(matrix):
    row = lax.broadcasted_iota(jnp.int32, matrix.shape, 0)
    lane = lax.broadcasted_iota(jnp.int32, matrix.shape, 1)
    return jnp.where(row == lane, matrix, 0.0)


def chain_kernel(red_ref, a_ref, b_ref, v_ref, d_ref, up_ref, na_ref, nb_ref, aug):
    width = a_ref.shape[1]
    cols = v_ref.shape[1]
    small = red_ref[656:696, :]
    gram_v = pltpu.roll(small, 64, 1)
    lower_inv = eliminate(with_identity(gram_v[:cols, :], 0))
    inv_v = dot(lower_inv, lower_inv, TN)
    vv = small[:cols, :cols]
    gram_r = gram_v[cols:cols + 8, :cols]
    gram_a = unpack_pair(red_ref, 0, red_ref[696:697, :])
    gram_b = unpack_pair(red_ref, 256, red_ref[697:698, :])
    va = jnp.concatenate([red_ref[512:512 + cols, :], red_ref[512 + cols:576, :]], axis=1)
    db = jnp.concatenate([red_ref[576:616, :], red_ref[616:656, :]], axis=1)
    proj_t, proj_r = db[:cols, :], db[cols:cols + 8, :]
    scale_a = 1.0 / jnp.maximum(largest(diagonal(gram_a)), largest(diagonal(vv)))
    scale_b = 1.0 / largest(diagonal(gram_b))
    gram_a = gram_a * scale_a
    va = va * scale_a
    vv = vv * scale_a

    w = dot(inv_v, proj_t)
    s = (gram_b - dot(proj_t, w, TN)) * scale_b
    ws = w * scale_b
    k1 = dot(gram_a, s) + dot(va, ws, TN)
    k2 = dot(va, s) + dot(vv, ws)
    j1 = dot(s, k1)
    c = dot(inv_v, k2)
    cs = c * scale_b
    aug[:, :width] = dot(k1, j1, TN) + dot(k2, cs, TN)
    row = lax.broadcasted_iota(jnp.int32, (width, width), 0)
    lane = lax.broadcasted_iota(jnp.int32, (width, width), 1)
    aug[:, width:] = jnp.where(row == lane, 1.0, 0.0)

    a, b, v, d = a_ref[...], b_ref[...], v_ref[...], d_ref[...]
    coeffs = -dot(gram_r, inv_v)
    lead = -proj_r - dot(coeffs, proj_t)
    up = dot(lead, a, NT) + dot(coeffs, v, NT)
    up_ref[...] = up[:1, :]
    root = jnp.sqrt(scale_b)
    fa = (dot(a, j1) + dot(v, cs)) / root
    fb = (dot(b - dot(d, w), k1) + dot(d, c)) * root

    for k in range(width // BLOCK):
        lo, hi = k * BLOCK, (k + 1) * BLOCK
        tile = lo // LANES * LANES
        linv = eliminate(with_identity(aug[lo:hi, tile:tile + LANES], lo - tile))
        rows = dot(linv, aug[lo:hi, :])
        aug[lo:hi, :] = rows
        if hi < width:
            below = rows[:, :width].T[hi:, :]
            aug[hi:, :] = aug[hi:, :] - dot(below, rows)
    inv = aug[:, width:]
    na_ref[...] = dot(fa, inv, NT)
    nb_ref[...] = dot(fb, inv, NT)


def finish(red, a, b, v, d):
    vmem = pl.BlockSpec(memory_space=pltpu.VMEM)
    rows, width = a.shape
    return pl.pallas_call(
        chain_kernel,
        out_shape=(
            jax.ShapeDtypeStruct((1, rows), jnp.float32),
            jax.ShapeDtypeStruct((rows, width), jnp.float32),
            jax.ShapeDtypeStruct((rows, width), jnp.float32),
        ),
        in_specs=[vmem] * 5,
        out_specs=(vmem,) * 3,
        scratch_shapes=[pltpu.VMEM((width, 2 * width), jnp.float32)],
        compiler_params=pltpu.CompilerParams(vmem_limit_bytes=32 << 20),
    )(red, a, b, v, d)


def solution(mesh):
    nx = mesh.shape["sub"]
    sizes = (mesh.shape["rows"] // (2 * nx), nx, nx)

    def on_device(a, b, v, d, r):
        red = reduce_all(sizes, a, b, v, d, r.reshape(1, -1))
        up, new_a, new_b = finish(red, a, b, v, d)
        return up.reshape(-1), new_a, new_b

    spread = P(("rows", "sub"))
    wide = P(("rows", "sub"), None)
    return jax.shard_map(
        on_device, mesh=mesh, in_specs=(wide,) * 4 + (spread,), out_specs=(spread, wide, wide), check_vma=False
    )
```

time: 967 us -> 81 us (0.08)
  waiting for transfers between devices: 460 us -> 0 us
  matrix products: 151 us -> 0 us
  other arithmetic: 141 us -> 0 us
  blocking collectives: 112 us -> 0 us
  Pallas kernels: 0 us -> 77.4 us
  local copies, waits for them, and re-layouts: 71.2 us -> 2.71 us
  between operations: 21.2 us -> 0.68 us
    psum x1 -> x0, waiting for transfers between devices: 460 us -> none  [on_device(): sent_a, sent_b = lax.psum((sent_a, sent_b), ('rows', 'sub'))]
    dot_general x814 -> x0, matrix products: 147 us -> none  [matmul(): jnp.dot(left, right, precision=lax.Precision.HIGHEST, preferred_element_t...]
    another operation x32 -> x0, other arithmetic: 135 us -> none  [the longest x11 48.2 us: truncate(): low_a = jnp.linalg.cholesky(gram_a)]
    psum x1 -> x0, blocking collectives: 112 us -> none  [on_device(): lax.psum((sent_v, proj, proj_r, gram_r), ('rows', 'sub'))]
    pallas_call x0 -> x2, Pallas kernels: none -> 77.4 us  [the longest x1 44.8 us: reduce_all(): pl.pallas_call(functools.partial(reduce_kernel, sizes), out_shape=jax.Sha...]
    gather x100 -> x0, local copies, waits for them, and re-layouts: 65.3 us -> none  [small_inverse(): diag_inv = 1.0 / jnp.diagonal(lower)]
  transfers between devices with their start and end apart: 1 -> 0, of which waited for: 1 -> 0; matrix products, arithmetic and copies ran while one was open for 0% -> 0% of each run, Pallas kernels for 0% -> 0%
where the time goes in v1:
time: 81 us; the launch traced here: 80.8 us
  Pallas kernels  77.4 us (96%)
  local copies, waits for them, and re-layouts  2.71 us (3%)
    pallas_call x1, Pallas kernels, reduce_all(): pl.pallas_call(functools.partial(reduce_kernel, sizes), out_shape=jax.Sha...  44.8 us
    pallas_call x1, Pallas kernels, finish(): pl.pallas_call(chain_kernel, out_shape=(jax.ShapeDtypeStruct((1, rows), j...  32.5 us
    unnamed x8, local copies, waits for them, and re-layouts  2.71 us

profile of v1, /device:TPU:1, one launch (start us, length us, event | category | flops | bytes accessed | tf_op | source)
XLA Modules:
  0.0 80.8 jit_solution(9724889498869763834)
XLA Ops:
  0.6 0.0 copy-start
  0.6 0.9 %copy.8.v_ref = f32[256,32]{1,0:T(8,128)S(1)} copy(f32[256,32]{0,1:T(8,128)} %param.7) | data formatting | bytes 65536 | tf_op args[2]
  1.5 0.0 copy-start.2
  1.5 0.9 %copy.9.d_ref = f32[256,32]{1,0:T(8,128)S(1)} copy(f32[256,32]{0,1:T(8,128)} %param.8) | data formatting | bytes 65536 | tf_op args[3]
  2.4 0.0 copy-done
  2.4 0.0 copy-done.2
  2.4 0.0 copy-start.1
  2.4 0.9 %copy-done.1 = f32[256,256]{1,0:T(8,128)S(1)} copy-done((f32[256,256]{1,0:T(8,128)S(1)}, f32[256,256]{1,0:T(8,128)}, u32[]{:S(2)}) %copy-start.1) | copy-done | bytes 262168
  3.4 44.8 %shard_map.76.red_ref = f32[768,128]{1,0:T(8,128)S(1)} custom-call(f32[256,256]{1,0:T(8,128)S(1)} %copy-done, f32[256,256]{1,0:T(8,128)S(1)} %copy-done.1, f32[256,32]{1,0:T(8,128)S(1)} %copy.8.v_ref, f32[256,32]{1,0:T(8,128)S(1)} %copy.9.d_ref, f32[1,256]{1,0:T(1,128)S(1)} %bitcast.2), custom_call_target="tpu_custom_call" | custom-call | tf_op jit(solution)/shard_map/pallas_call | solution.py:195
  48.2 32.5 %shard_map.77 = (f32[1,256]{1,0:T(1,128)}, f32[256,256]{1,0:T(8,128)}, f32[256,256]{1,0:T(8,128)}) custom-call(f32[768,128]{1,0:T(8,128)S(1)} %shard_map.76.red_ref, f32[256,256]{1,0:T(8,128)S(1)} %copy-done, f32[256,256]{1,0:T(8,128)S(1)} %copy-done.1, f32[256,32]{1,0:T(8,128)S(1)} %copy.8.v_ref, f32[256,32]{1,0:T(8,128)S(1)} %copy.9.d_ref), custom_call_target="tpu_custom_call" | custom-call | tf_op jit(solution)/shard_map/pallas_call | solution.py:303
Async XLA Ops:
  0.6 1.8 %copy-start = (f32[256,256]{1,0:T(8,128)S(1)}, f32[256,256]{1,0:T(8,128)}, u32[]{:S(2)}) copy-start(f32[256,256]{1,0:T(8,128)} %a_ref.3) | copy-start | bytes 786436
  1.5 0.9 %copy-start.2 = (f32[256]{0:T(256)S(1)}, f32[256]{0:T(256)}, u32[]{:S(2)}) copy-start(f32[256]{0:T(256)} %param.9) | copy-start | bytes 3076
  2.4 1.0 %copy-start.1 = (f32[256,256]{1,0:T(8,128)S(1)}, f32[256,256]{1,0:T(8,128)}, u32[]{:S(2)}) copy-start(f32[256,256]{1,0:T(8,128)} %b_ref.3) | copy-start | bytes 786436

commit v2 on v1

--- a/solution.py
+++ b/solution.py
@@ -81,14 +81,14 @@
 
     a, b = a_ref[...], b_ref[...]
     v, d = v_ref[...], d_ref[...]
-    cols = v.shape[1]
+    cols = v.shape[0]
     diag_a = pack_pair(dot(a, a, TN), local, 0)
     diag_b = pack_pair(dot(b, b, TN), local, 2 * LANES)
-    va = dot(v, a, TN)
-    left = jnp.concatenate([d.T, jnp.broadcast_to(r_ref[...], (8, d.shape[0]))], axis=0)
+    va = dot(v, a)
+    left = jnp.concatenate([d, jnp.broadcast_to(r_ref[...], (8, d.shape[1]))], axis=0)
     db = dot(left, b)
-    dd = dot(left, d)
-    vv = dot(v, v, TN)
+    dd = dot(left, d, NT)
+    vv = dot(v, v, NT)
     local[512:512 + cols, :] = va[:, :LANES]
     local[512 + cols:576, :] = va[:, LANES:]
     local[576:616, :] = db[:, :LANES]
@@ -213,22 +213,31 @@
     )(a, b, v, d, r)
 
 
-def eliminate(block):
-    row = lax.broadcasted_iota(jnp.int32, (BLOCK, LANES), 0)
+def inverse_factor(tile, lane_in, lane_out):
+    groups = BLOCK // 8
+    sub = lax.broadcasted_iota(jnp.int32, (8, LANES), 0)
+    lane = lax.broadcasted_iota(jnp.int32, (8, LANES), 1)
+    columns = [
+        {
+            i: jnp.broadcast_to(tile[8 * i:8 * i + 8, lane_in + j:lane_in + j + 1], (8, LANES))
+            for i in range(j // 8, groups)
+        }
+        for j in range(BLOCK)
+    ]
+    out = [jnp.where(lane == sub + (8 * i + lane_out), 1.0, 0.0) for i in range(groups)]
     for j in range(BLOCK):
-        scale = lax.rsqrt(block[j:j + 1, j:j + 1])
-        pivot = block[j:j + 1, :] * scale
-        column = block[:, j:j + 1] * scale
-        block = jnp.where(row > j, block - column * pivot, jnp.where(row == j, pivot, block))
-    return pltpu.roll(block, LANES - BLOCK, 1)[:, :BLOCK]
-
-
-def with_identity(block, offset):
-    row = lax.broadcasted_iota(jnp.int32, (BLOCK, LANES), 0)
-    lane = lax.broadcasted_iota(jnp.int32, (BLOCK, LANES), 1)
-    if offset:
-        block = pltpu.roll(block, LANES - offset, 1)
-    return jnp.where(lane < BLOCK, block, jnp.where(lane == row + BLOCK, 1.0, 0.0))
+        g, r = j // 8, j % 8
+        scale = lax.rsqrt(columns[j][g][r:r + 1, :])
+        column = {i: columns[j][i] * scale for i in range(g, groups)}
+        pivot = out[g][r:r + 1, :] * scale
+        for b in range(j + 1, BLOCK):
+            factor = column[b // 8][b % 8:b % 8 + 1, :]
+            for i in range(b // 8, groups):
+                columns[b][i] = columns[b][i] - column[i] * factor
+        out[g] = jnp.where(sub > r, out[g] - column[g] * pivot, jnp.where(sub == r, pivot, out[g]))
+        for i in range(g + 1, groups):
+            out[i] = out[i] - column[i] * pivot
+    return jnp.concatenate(out, axis=0)
 
 
 def largest(values):
@@ -241,15 +250,23 @@
     return jnp.where(row == lane, matrix, 0.0)
 
 
-def chain_kernel(red_ref, a_ref, b_ref, v_ref, d_ref, up_ref, na_ref, nb_ref, aug):
-    width = a_ref.shape[1]
-    cols = v_ref.shape[1]
+def framed(rows, before, after):
+    parts = [rows]
+    if before:
+        parts = [jnp.zeros((before, rows.shape[1]), rows.dtype)] + parts
+    if after:
+        parts = parts + [jnp.zeros((after, rows.shape[1]), rows.dtype)]
+    return jnp.concatenate(parts, axis=0) if len(parts) > 1 else rows
+
+
+def chain_kernel(red_ref, a_ref, b_ref, v_ref, d_ref, up_ref, na_ref, nb_ref, z_ref, f_ref):
+    rows, width = a_ref.shape
+    cols = v_ref.shape[0]
     small = red_ref[656:696, :]
-    gram_v = pltpu.roll(small, 64, 1)
-    lower_inv = eliminate(with_identity(gram_v[:cols, :], 0))
-    inv_v = dot(lower_inv, lower_inv, TN)
+    lower_inv = inverse_factor(small[:cols, :], 64, 0)[:, :cols]
+    inv_v = dot(lower_inv.T, lower_inv)
     vv = small[:cols, :cols]
-    gram_r = gram_v[cols:cols + 8, :cols]
+    gram_r = small[cols:cols + 8, 64:64 + cols]
     gram_a = unpack_pair(red_ref, 0, red_ref[696:697, :])
     gram_b = unpack_pair(red_ref, 256, red_ref[697:698, :])
     va = jnp.concatenate([red_ref[512:512 + cols, :], red_ref[512 + cols:576, :]], axis=1)
@@ -260,41 +277,57 @@
     gram_a = gram_a * scale_a
     va = va * scale_a
     vv = vv * scale_a
+    av = va.T
+    proj = proj_t.T
 
     w = dot(inv_v, proj_t)
-    s = (gram_b - dot(proj_t, w, TN)) * scale_b
     ws = w * scale_b
-    k1 = dot(gram_a, s) + dot(va, ws, TN)
+    wst = dot(proj, inv_v) * scale_b
+    s = (gram_b - dot(proj, w)) * scale_b
+    k1 = dot(gram_a, s) + dot(av, ws)
+    k1t = dot(s, gram_a) + dot(wst, va)
     k2 = dot(va, s) + dot(vv, ws)
+    k2t = dot(s, av) + dot(wst, vv)
     j1 = dot(s, k1)
     c = dot(inv_v, k2)
     cs = c * scale_b
-    aug[:, :width] = dot(k1, j1, TN) + dot(k2, cs, TN)
-    row = lax.broadcasted_iota(jnp.int32, (width, width), 0)
-    lane = lax.broadcasted_iota(jnp.int32, (width, width), 1)
-    aug[:, width:] = jnp.where(row == lane, 1.0, 0.0)
-
-    a, b, v, d = a_ref[...], b_ref[...], v_ref[...], d_ref[...]
+    z_ref[...] = dot(k1t, j1) + dot(k2t, cs)
+
+    a, b = a_ref[...], b_ref[...]
+    v, d = v_ref[...], d_ref[...]
     coeffs = -dot(gram_r, inv_v)
     lead = -proj_r - dot(coeffs, proj_t)
-    up = dot(lead, a, NT) + dot(coeffs, v, NT)
+    up = dot(lead, a, NT) + dot(coeffs, v)
     up_ref[...] = up[:1, :]
     root = jnp.sqrt(scale_b)
-    fa = (dot(a, j1) + dot(v, cs)) / root
-    fb = (dot(b - dot(d, w), k1) + dot(d, c)) * root
-
-    for k in range(width // BLOCK):
-        lo, hi = k * BLOCK, (k + 1) * BLOCK
-        tile = lo // LANES * LANES
-        linv = eliminate(with_identity(aug[lo:hi, tile:tile + LANES], lo - tile))
-        rows = dot(linv, aug[lo:hi, :])
-        aug[lo:hi, :] = rows
+    f_ref[:rows, :] = (dot(a, j1) + dot(v.T, cs)) / root
+    dn = d.T
+    f_ref[rows:, :] = (dot(b - dot(dn, w), k1) + dot(dn, c)) * root
+
+    for lo in range(0, width, BLOCK):
+        hi = lo + BLOCK
+        base = lo // LANES * LANES
+        tile = slice(base, base + LANES)
+        inv = inverse_factor(z_ref[lo:hi, tile], lo - base, lo - base)
+        inv = framed(inv, lo - base, base + LANES - hi)
         if hi < width:
-            below = rows[:, :width].T[hi:, :]
-            aug[hi:, :] = aug[hi:, :] - dot(below, rows)
-    inv = aug[:, width:]
-    na_ref[...] = dot(fa, inv, NT)
-    nb_ref[...] = dot(fb, inv, NT)
+            panel = dot(z_ref[hi:, tile], inv, NT)
+            for start in range(hi // LANES * LANES, width, LANES):
+                first = max(hi, start)
+                right = framed(panel[first - hi:start + LANES - hi, :], first - start, 0)
+                z_ref[first:, start:start + LANES] = z_ref[first:, start:start + LANES] - dot(panel[first - hi:, :], right, NT)
+        done = dot(f_ref[:, tile], inv, NT)
+        if lo == base:
+            na_ref[:, tile] = done[:rows, :]
+            nb_ref[:, tile] = done[rows:, :]
+        else:
+            na_ref[:, tile] = na_ref[:, tile] + done[:rows, :]
+            nb_ref[:, tile] = nb_ref[:, tile] + done[rows:, :]
+        if hi < width:
+            for start in range(hi // LANES * LANES, width, LANES):
+                first = max(hi, start)
+                right = framed(panel[first - hi:start + LANES - hi, :], first - start, 0)
+                f_ref[:, start:start + LANES] = f_ref[:, start:start + LANES] - dot(done, right, NT)
 
 
 def finish(red, a, b, v, d):
@@ -309,7 +342,7 @@
         ),
         in_specs=[vmem] * 5,
         out_specs=(vmem,) * 3,
-        scratch_shapes=[pltpu.VMEM((width, 2 * width), jnp.float32)],
+        scratch_shapes=[pltpu.VMEM((width, width), jnp.float32), pltpu.VMEM((2 * rows, width), jnp.float32)],
         compiler_params=pltpu.CompilerParams(vmem_limit_bytes=32 << 20),
     )(red, a, b, v, d)
 
@@ -319,8 +352,8 @@
     sizes = (mesh.shape["rows"] // (2 * nx), nx, nx)
 
     def on_device(a, b, v, d, r):
-        red = reduce_all(sizes, a, b, v, d, r.reshape(1, -1))
-        up, new_a, new_b = finish(red, a, b, v, d)
+        red = reduce_all(sizes, a, b, v.T, d.T, r.reshape(1, -1))
+        up, new_a, new_b = finish(red, a, b, v.T, d.T)
         return up.reshape(-1), new_a, new_b
 
     spread = P(("rows", "sub"))

time: 81 us -> 64.6 us (0.80)
  Pallas kernels: 77.4 us -> 59.6 us
  local copies, waits for them, and re-layouts: 2.71 us -> 4.09 us
    pallas_call x1, Pallas kernels: 32.5 us -> 14.7 us  [finish(): pl.pallas_call(chain_kernel, out_shape=(jax.ShapeDtypeStruct((1, rows), j...]
    unnamed x8 -> x10, local copies, waits for them, and re-layouts: 2.71 us -> 4.09 us
where the time goes in v2:
time: 64.6 us; the launch traced here: 64.3 us
  Pallas kernels  59.6 us (92%)
  local copies, waits for them, and re-layouts  4.09 us (6%)
  between operations  0.65 us (1%)
    pallas_call x1, Pallas kernels, reduce_all(): pl.pallas_call(functools.partial(reduce_kernel, sizes), out_shape=jax.Sha...  44.8 us
    pallas_call x1, Pallas kernels, finish(): pl.pallas_call(chain_kernel, out_shape=(jax.ShapeDtypeStruct((1, rows), j...  14.7 us
    unnamed x10, local copies, waits for them, and re-layouts  4.09 us

profile of v2, /device:TPU:1, one launch (start us, length us, event | category | flops | bytes accessed | tf_op | source)
XLA Modules:
  0.0 64.3 jit_solution(2269442038274063944)
XLA Ops:
  0.6 0.0 copy-start.4
  0.6 0.7 %copy-done.4 = f32[256]{0:T(256)S(1)} copy-done((f32[256]{0:T(256)S(1)}, f32[256]{0:T(256)}, u32[]{:S(2)}) %copy-start.4) | copy-done | bytes 1048
  1.3 0.0 copy-start
  1.3 0.9 %copy-done = f32[256,256]{1,0:T(8,128)S(1)} copy-done((f32[256,256]{1,0:T(8,128)S(1)}, f32[256,256]{1,0:T(8,128)}, u32[]{:S(2)}) %copy-start) | copy-done | bytes 262168
  2.3 0.0 copy-start.1
  2.3 0.9 %copy-done.1 = f32[256,256]{1,0:T(8,128)S(1)} copy-done((f32[256,256]{1,0:T(8,128)S(1)}, f32[256,256]{1,0:T(8,128)}, u32[]{:S(2)}) %copy-start.1) | copy-done | bytes 262168
  3.2 0.0 copy-start.2
  3.2 0.8 %copy-done.2 = f32[256,32]{0,1:T(8,128)S(1)} copy-done((f32[256,32]{0,1:T(8,128)S(1)}, f32[256,32]{0,1:T(8,128)}, u32[]{:S(2)}) %copy-start.2) | copy-done | bytes 32792
  4.0 0.0 copy-start.3
  4.0 0.8 %copy-done.3 = f32[256,32]{0,1:T(8,128)S(1)} copy-done((f32[256,32]{0,1:T(8,128)S(1)}, f32[256,32]{0,1:T(8,128)}, u32[]{:S(2)}) %copy-start.3) | copy-done | bytes 32792
  4.7 44.8 %shard_map.76.red_ref = f32[768,128]{1,0:T(8,128)S(1)} custom-call(f32[256,256]{1,0:T(8,128)S(1)} %copy-done, f32[256,256]{1,0:T(8,128)S(1)} %copy-done.1, f32[32,256]{1,0:T(8,128)S(1)} %bitcast.4, f32[32,256]{1,0:T(8,128)S(1)} %bitcast.6, f32[1,256]{1,0:T(1,128)S(1)} %bitcast.8), custom_call_target="tpu_custom_call" | custom-call | tf_op jit(solution)/shard_map/pallas_call | solution.py:195
  49.6 14.7 %shard_map.77 = (f32[1,256]{1,0:T(1,128)}, f32[256,256]{1,0:T(8,128)}, f32[256,256]{1,0:T(8,128)}) custom-call(f32[768,128]{1,0:T(8,128)S(1)} %shard_map.76.red_ref, f32[256,256]{1,0:T(8,128)S(1)} %copy-done, f32[256,256]{1,0:T(8,128)S(1)} %copy-done.1, f32[32,256]{1,0:T(8,128)S(1)} %bitcast.5, f32[32,256]{1,0:T(8,128)S(1)} %bitcast.7), custom_call_target="tpu_custom_call" | custom-call | tf_op jit(solution)/shard_map/pallas_call | solution.py:336
Async XLA Ops:
  0.6 0.7 %copy-start.4 = (f32[256]{0:T(256)S(1)}, f32[256]{0:T(256)}, u32[]{:S(2)}) copy-start(f32[256]{0:T(256)} %param.9) | copy-start | bytes 3076
  1.3 0.9 %copy-start = (f32[256,256]{1,0:T(8,128)S(1)}, f32[256,256]{1,0:T(8,128)}, u32[]{:S(2)}) copy-start(f32[256,256]{1,0:T(8,128)} %a_ref.3) | copy-start | bytes 786436
  2.3 0.9 %copy-start.1 = (f32[256,256]{1,0:T(8,128)S(1)}, f32[256,256]{1,0:T(8,128)}, u32[]{:S(2)}) copy-start(f32[256,256]{1,0:T(8,128)} %b_ref.3) | copy-start | bytes 786436
  3.2 0.8 %copy-start.2 = (f32[256,32]{0,1:T(8,128)S(1)}, f32[256,32]{0,1:T(8,128)}, u32[]{:S(2)}) copy-start(f32[256,32]{0,1:T(8,128)} %param.7) | copy-start | bytes 98308
  4.0 0.8 %copy-start.3 = (f32[256,32]{0,1:T(8,128)S(1)}, f32[256,32]{0,1:T(8,128)}, u32[]{:S(2)}) copy-start(f32[256,32]{0,1:T(8,128)} %param.8) | copy-start | bytes 98308

commit v3 on v2

--- a/solution.py
+++ b/solution.py
@@ -17,16 +17,35 @@
 TN = (((0,), (0,)), ((), ()))
 
 
+def halves(value):
+    high = value.astype(jnp.bfloat16)
+    return high, (value - high.astype(jnp.float32)).astype(jnp.bfloat16)
+
+
 def dot(left, right, dims=NN):
-    return lax.dot_general(left, right, dims, precision=lax.Precision.HIGHEST, preferred_element_type=jnp.float32)
-
-
-def pack_pair(gram, out_ref, base):
+    left = left if isinstance(left, tuple) else halves(left)
+    right = right if isinstance(right, tuple) else halves(right)
+
+    def one(l, r):
+        return lax.dot_general(l, r, dims, preferred_element_type=jnp.float32)
+
+    return one(left[0], right[0]) + (one(left[0], right[1]) + one(left[1], right[0]))
+
+
+def gram_pair(value, out_ref, base):
+    turned = value.T
+    whole, first = halves(value), halves(turned[:LANES, :])
+    return pack_pair(
+        dot(first, tuple(part[:, :LANES] for part in whole)), dot(turned[LANES:, :], whole), out_ref, base
+    )
+
+
+def pack_pair(first, below, out_ref, base):
     row = lax.broadcasted_iota(jnp.int32, (LANES, LANES), 0)
     lane = lax.broadcasted_iota(jnp.int32, (LANES, LANES), 1)
-    first, last = gram[:LANES, :LANES], gram[LANES:, LANES:]
+    last = below[:, LANES:]
     out_ref[base:base + LANES, :] = jnp.where(row >= lane, first, last)
-    out_ref[base + LANES:base + 2 * LANES, :] = gram[LANES:, :LANES]
+    out_ref[base + LANES:base + 2 * LANES, :] = below[:, :LANES]
     return jnp.sum(jnp.where(row == lane, last, 0.0), axis=0, keepdims=True)
 
 
@@ -43,7 +62,14 @@
     )
 
 
-def reduce_kernel(sizes, a_ref, b_ref, v_ref, d_ref, r_ref, out_ref, local, pair, half, near, mine, far, total, full,
+def fetch(sources, targets, sems):
+    copies = [pltpu.make_async_copy(src, dst, sems.at[k]) for k, (src, dst) in enumerate(zip(sources, targets))]
+    for copy in copies:
+        copy.start()
+    return copies
+
+
+def reduce_kernel(sizes, a_hbm, b_hbm, v_hbm, d_hbm, r_hbm, out_ref, a_ref, b_ref, v_ref, d_ref, r_ref, load_sem, local, pair, half, near, mine, far, total, full,
                   pair_sem, near_sem, far_sem, total_sem, back_sem, cross_sem,
                   pair_out, near_out, far_out, total_out, back_out, cross_out):
     nz, ny, nx = sizes
@@ -72,6 +98,7 @@
     partner = (place + 1 - 2 * core, x)
     owners = [(t * nz) // tiles if nz >= tiles else t % nz for t in range(tiles)]
 
+    loads = fetch((b_hbm, d_hbm, r_hbm, a_hbm, v_hbm), (b_ref, d_ref, r_ref, a_ref, v_ref), load_sem)
     barrier = pltpu.get_barrier_semaphore()
     for _, _, dev in far_ids:
         pl.semaphore_signal(barrier, inc=1, device_id=dev, device_id_type=MESH)
@@ -79,15 +106,19 @@
         pl.semaphore_signal(barrier, inc=1, device_id=dev, device_id_type=MESH)
     pl.semaphore_signal(barrier, inc=1, device_id=partner, device_id_type=MESH)
 
-    a, b = a_ref[...], b_ref[...]
-    v, d = v_ref[...], d_ref[...]
-    cols = v.shape[0]
-    diag_a = pack_pair(dot(a, a, TN), local, 0)
-    diag_b = pack_pair(dot(b, b, TN), local, 2 * LANES)
-    va = dot(v, a)
-    left = jnp.concatenate([d, jnp.broadcast_to(r_ref[...], (8, d.shape[1]))], axis=0)
-    db = dot(left, b)
+    cols = v_ref.shape[0]
+    for copy in loads[:3]:
+        copy.wait()
+    diag_b = gram_pair(b_ref[...], local, 2 * LANES)
+    d = d_ref[...]
+    left = halves(jnp.concatenate([d, jnp.broadcast_to(r_ref[...], (8, d.shape[1]))], axis=0))
+    db = dot(left, b_ref[...])
     dd = dot(left, d, NT)
+    for copy in loads[3:]:
+        copy.wait()
+    diag_a = gram_pair(a_ref[...], local, 0)
+    v = halves(v_ref[...])
+    va = dot(v, a_ref[...])
     vv = dot(v, v, NT)
     local[512:512 + cols, :] = va[:, :LANES]
     local[512 + cols:576, :] = va[:, LANES:]
@@ -195,9 +226,11 @@
     return pl.pallas_call(
         functools.partial(reduce_kernel, sizes),
         out_shape=jax.ShapeDtypeStruct((PACK, LANES), jnp.float32),
-        in_specs=[vmem] * 5,
+        in_specs=[pl.BlockSpec(memory_space=pltpu.HBM)] * 5,
         out_specs=vmem,
         scratch_shapes=[
+            *(pltpu.VMEM(value.shape, jnp.float32) for value in (a, b, v, d, r)),
+            dma((5,)),
             pltpu.VMEM((PACK, LANES), jnp.float32),
             pltpu.VMEM((PACK // 2, LANES), jnp.float32),
             pltpu.VMEM((PACK // 2, LANES), jnp.float32),
@@ -259,7 +292,8 @@
     return jnp.concatenate(parts, axis=0) if len(parts) > 1 else rows
 
 
-def chain_kernel(red_ref, a_ref, b_ref, v_ref, d_ref, up_ref, na_ref, nb_ref, z_ref, f_ref):
+def chain_kernel(red_ref, a_hbm, b_hbm, v_hbm, d_hbm, up_ref, na_ref, nb_ref, a_ref, b_ref, v_ref, d_ref, load_sem, z_ref, f_ref):
+    loads = fetch((a_hbm, b_hbm, v_hbm, d_hbm), (a_ref, b_ref, v_ref, d_ref), load_sem)
     rows, width = a_ref.shape
     cols = v_ref.shape[0]
     small = red_ref[656:696, :]
@@ -280,42 +314,49 @@
     av = va.T
     proj = proj_t.T
 
+    inv_v = halves(inv_v)
     w = dot(inv_v, proj_t)
-    ws = w * scale_b
-    wst = dot(proj, inv_v) * scale_b
-    s = (gram_b - dot(proj, w)) * scale_b
-    k1 = dot(gram_a, s) + dot(av, ws)
+    proj = halves(proj)
+    wt = dot(proj, inv_v)
+    ws = halves(w * scale_b)
+    wst = halves(wt * scale_b)
+    s = halves((gram_b - dot(proj, w)) * scale_b)
+    gram_a, va, vv, av = halves(gram_a), halves(va), halves(vv), halves(av)
+    k1 = halves(dot(gram_a, s) + dot(av, ws))
     k1t = dot(s, gram_a) + dot(wst, va)
     k2 = dot(va, s) + dot(vv, ws)
     k2t = dot(s, av) + dot(wst, vv)
-    j1 = dot(s, k1)
+    j1 = halves(dot(s, k1))
     c = dot(inv_v, k2)
-    cs = c * scale_b
+    cs = halves(c * scale_b)
     z_ref[...] = dot(k1t, j1) + dot(k2t, cs)
 
-    a, b = a_ref[...], b_ref[...]
+    for copy in loads:
+        copy.wait()
     v, d = v_ref[...], d_ref[...]
     coeffs = -dot(gram_r, inv_v)
     lead = -proj_r - dot(coeffs, proj_t)
+    a = halves(a_ref[...])
     up = dot(lead, a, NT) + dot(coeffs, v)
     up_ref[...] = up[:1, :]
     root = jnp.sqrt(scale_b)
     f_ref[:rows, :] = (dot(a, j1) + dot(v.T, cs)) / root
-    dn = d.T
-    f_ref[rows:, :] = (dot(b - dot(dn, w), k1) + dot(dn, c)) * root
+    dn = halves(d.T)
+    f_ref[rows:, :] = (dot(b_ref[...] - dot(dn, w), k1) + dot(dn, c)) * root
 
     for lo in range(0, width, BLOCK):
         hi = lo + BLOCK
         base = lo // LANES * LANES
         tile = slice(base, base + LANES)
         inv = inverse_factor(z_ref[lo:hi, tile], lo - base, lo - base)
-        inv = framed(inv, lo - base, base + LANES - hi)
+        inv = halves(framed(inv, lo - base, base + LANES - hi))
         if hi < width:
-            panel = dot(z_ref[hi:, tile], inv, NT)
+            panel = halves(dot(z_ref[hi:, tile], inv, NT))
             for start in range(hi // LANES * LANES, width, LANES):
                 first = max(hi, start)
-                right = framed(panel[first - hi:start + LANES - hi, :], first - start, 0)
-                z_ref[first:, start:start + LANES] = z_ref[first:, start:start + LANES] - dot(panel[first - hi:, :], right, NT)
+                left = tuple(part[first - hi:, :] for part in panel)
+                right = tuple(framed(part[first - hi:start + LANES - hi, :], first - start, 0) for part in panel)
+                z_ref[first:, start:start + LANES] = z_ref[first:, start:start + LANES] - dot(left, right, NT)
         done = dot(f_ref[:, tile], inv, NT)
         if lo == base:
             na_ref[:, tile] = done[:rows, :]
@@ -324,9 +365,10 @@
             na_ref[:, tile] = na_ref[:, tile] + done[:rows, :]
             nb_ref[:, tile] = nb_ref[:, tile] + done[rows:, :]
         if hi < width:
+            done = halves(done)
             for start in range(hi // LANES * LANES, width, LANES):
                 first = max(hi, start)
-                right = framed(panel[first - hi:start + LANES - hi, :], first - start, 0)
+                right = tuple(framed(part[first - hi:start + LANES - hi, :], first - start, 0) for part in panel)
                 f_ref[:, start:start + LANES] = f_ref[:, start:start + LANES] - dot(done, right, NT)
 
 
@@ -340,9 +382,12 @@
             jax.ShapeDtypeStruct((rows, width), jnp.float32),
             jax.ShapeDtypeStruct((rows, width), jnp.float32),
         ),
-        in_specs=[vmem] * 5,
+        in_specs=[vmem] + [pl.BlockSpec(memory_space=pltpu.HBM)] * 4,
         out_specs=(vmem,) * 3,
-        scratch_shapes=[pltpu.VMEM((width, width), jnp.float32), pltpu.VMEM((2 * rows, width), jnp.float32)],
+        scratch_shapes=[
+            *(pltpu.VMEM(value.shape, jnp.float32) for value in (a, b, v, d)),
+            pltpu.SemaphoreType.DMA((4,)),
+            pltpu.VMEM((width, width), jnp.float32), pltpu.VMEM((2 * rows, width), jnp.float32)],
         compiler_params=pltpu.CompilerParams(vmem_limit_bytes=32 << 20),
     )(red, a, b, v, d)
 
@@ -352,8 +397,10 @@
     sizes = (mesh.shape["rows"] // (2 * nx), nx, nx)
 
     def on_device(a, b, v, d, r):
-        red = reduce_all(sizes, a, b, v.T, d.T, r.reshape(1, -1))
-        up, new_a, new_b = finish(red, a, b, v.T, d.T)
+        hbm = lambda value: pltpu.with_memory_space_constraint(value, pltpu.HBM)
+        a, b, vt, dt, rt = hbm(a), hbm(b), hbm(v.T), hbm(d.T), hbm(r.reshape(1, -1))
+        red = reduce_all(sizes, a, b, vt, dt, rt)
+        up, new_a, new_b = finish(red, a, b, vt, dt)
         return up.reshape(-1), new_a, new_b
 
     spread = P(("rows", "sub"))

time: 64.6 us -> 57.6 us (0.89)
  local copies, waits for them, and re-layouts: 4.09 us -> 0 us
  Pallas kernels: 59.6 us -> 56.8 us
    unnamed x10 -> x0, local copies, waits for them, and re-layouts: 4.09 us -> none
    pallas_call x1, Pallas kernels: 14.7 us -> 12 us  [finish(): pl.pallas_call(chain_kernel, out_shape=(jax.ShapeDtypeStruct((1, rows), j...]
where the time goes in v3:
time: 57.6 us; the launch traced here: 57.5 us
  Pallas kernels  56.8 us (99%)
  between operations  0.64 us (1%)
    pallas_call x1, Pallas kernels, reduce_all(): pl.pallas_call(functools.partial(reduce_kernel, sizes), out_shape=jax.Sha...  44.9 us
    pallas_call x1, Pallas kernels, finish(): pl.pallas_call(chain_kernel, out_shape=(jax.ShapeDtypeStruct((1, rows), j...  12 us

profile of v3, /device:TPU:1, one launch (start us, length us, event | category | flops | bytes accessed | tf_op | source)
XLA Modules:
  0.0 57.5 jit_solution(3206417896950502170)
XLA Ops:
  0.6 44.9 %shard_map.76.red_ref = f32[768,128]{1,0:T(8,128)S(1)} custom-call(f32[256,256]{1,0:T(8,128)} %a_hbm.3, f32[256,256]{1,0:T(8,128)} %b_hbm.3, f32[32,256]{1,0:T(8,128)} %bitcast.4, f32[32,256]{1,0:T(8,128)} %bitcast.6, f32[1,256]{1,0:T(1,128)} %bitcast.8), custom_call_target="tpu_custom_call" | custom-call | tf_op jit(solution)/shard_map/pallas_call | solution.py:226
  45.5 12.0 %shard_map.77 = (f32[1,256]{1,0:T(1,128)}, f32[256,256]{1,0:T(8,128)}, f32[256,256]{1,0:T(8,128)}) custom-call(f32[768,128]{1,0:T(8,128)S(1)} %shard_map.76.red_ref, f32[256,256]{1,0:T(8,128)} %a_hbm.3, f32[256,256]{1,0:T(8,128)} %b_hbm.3, f32[32,256]{1,0:T(8,128)} %bitcast.5, f32[32,256]{1,0:T(8,128)} %bitcast.7), custom_call_target="tpu_custom_call" | custom-call | tf_op jit(solution)/shard_map/pallas_call | solution.py:378

commit v4 on v3

--- a/solution.py
+++ b/solution.py
@@ -9,7 +9,7 @@
 
 MESH = pl.DeviceIdType.MESH
 LANES = 128
-PACK = 768
+PACK = 704
 BLOCK = 32
 
 NN = (((1,), (0,)), ((), ()))
@@ -69,38 +69,46 @@
     return copies
 
 
-def reduce_kernel(sizes, a_hbm, b_hbm, v_hbm, d_hbm, r_hbm, out_ref, a_ref, b_ref, v_ref, d_ref, r_ref, load_sem, local, pair, half, near, mine, far, total, full,
-                  pair_sem, near_sem, far_sem, total_sem, back_sem, cross_sem,
-                  pair_out, near_out, far_out, total_out, back_out, cross_out):
+def reduce_kernel(sizes, a_hbm, b_hbm, v_hbm, d_hbm, r_hbm, out_ref, a_ref, b_ref, v_ref, d_ref, r_ref, load_sem,
+                  local, pair, half, near, more, mine, far, total, full,
+                  pair_sem, near_sem, more_sem, far_sem, back_sem, rest_sem, cross_sem,
+                  pair_out, near_out, more_out, far_out, back_out, rest_out, cross_out):
     nz, ny, nx = sizes
-    peers = ny * nx
     rows = PACK // 2
-    piece = rows // peers
-    tiles = piece // 8
+    plane = ny * nx
+    cell = 2 * plane
+    steps = nz // 2
     place = lax.axis_index("rows")
     x = lax.axis_index("sub")
     core = lax.rem(place, 2)
     y = lax.rem(place // 2, ny)
     z = place // (2 * ny)
-    me = y * nx + x
+    side, step = lax.rem(z, 2), z // 2
+    me = side * plane + y * nx + x
     near_ids = []
-    for dy in range(ny):
-        for dx in range(nx):
-            if dy or dx:
-                qy, qx = lax.rem(y + dy, ny), lax.rem(x + dx, nx)
-                hops = min(dy, ny - dy) + min(dx, nx - dx)
-                near_ids.append((hops, dy * nx + dx, qy * nx + qx, ((z * ny + qy) * 2 + core, qx)))
+    for dz in range(2):
+        for dy in range(ny):
+            for dx in range(nx):
+                if dz or dy or dx:
+                    qz, qy, qx = lax.rem(side + dz, 2), lax.rem(y + dy, ny), lax.rem(x + dx, nx)
+                    hops = dz + min(dy, ny - dy) + min(dx, nx - dx)
+                    dev = (((2 * step + qz) * ny + qy) * 2 + core, qx)
+                    near_ids.append((hops, len(near_ids), qz * plane + qy * nx + qx, dev))
     near_ids = [item[2:] for item in sorted(near_ids, key=lambda item: (-item[0], item[1]))]
     far_ids = []
-    for dz in sorted(range(1, nz), key=lambda d: -min(d, nz - d)):
-        qz = lax.rem(z + dz, nz)
-        far_ids.append((dz, qz, ((qz * ny + y) * 2 + core, x)))
+    for dz in sorted(range(1, steps), key=lambda d: -min(d, steps - d)):
+        qz = lax.rem(step + dz, steps)
+        far_ids.append((qz, ((2 * (2 * ny) * qz + 2 * ny * side) + 2 * y + core, x)))
     partner = (place + 1 - 2 * core, x)
-    owners = [(t * nz) // tiles if nz >= tiles else t % nz for t in range(tiles)]
+    doubles = [(0, qy, qx) for qy in range(ny) for qx in range(nx) if (qx + qy) % 2 == 0]
+    doubles += [(1, qy, qx) for qy in range(ny) for qx in range(nx) if (qx + qy) % 4 == 1]
+    even = side == 0
+    double = (even & (lax.rem(x + y, 2) == 0)) | ((side == 1) & (lax.rem(x + y, 4) == 1))
+    mine_second = jnp.where(even, y * (nx // 2) + x // 2, plane // 2 + y)
 
     loads = fetch((b_hbm, d_hbm, r_hbm, a_hbm, v_hbm), (b_ref, d_ref, r_ref, a_ref, v_ref), load_sem)
     barrier = pltpu.get_barrier_semaphore()
-    for _, _, dev in far_ids:
+    for _, dev in far_ids:
         pl.semaphore_signal(barrier, inc=1, device_id=dev, device_id_type=MESH)
     for _, dev in near_ids:
         pl.semaphore_signal(barrier, inc=1, device_id=dev, device_id_type=MESH)
@@ -127,7 +135,7 @@
     local[656:696, :] = jnp.zeros((40, LANES), jnp.float32)
     local[656:656 + cols, 0:cols] = vv
     local[656:696, 64:64 + cols] = dd
-    local[696:768, :] = jnp.zeros((72, LANES), jnp.float32)
+    local[696:704, :] = jnp.zeros((8, LANES), jnp.float32)
     local[696:697, :] = diag_a
     local[697:698, :] = diag_b
 
@@ -145,82 +153,110 @@
 
     pending = []
 
-    def ds(start, size):
+    def at(start, size=8):
         return pl.ds(pl.multiple_of(start, 8), size)
 
-    pending.append(send(local.at[ds((1 - core) * rows, rows)], pair, pair_out, pair_sem, partner))
+    def each_double(action):
+        for k, (qz, qy, qx) in enumerate(doubles):
+
+            @pl.when(me != qz * plane + qy * nx + qx)
+            def _():
+                action(k, (((2 * step + qz) * ny + qy) * 2 + core, qx))
+
+    pending.append(send(local.at[at((1 - core) * rows, rows)], pair, pair_out, pair_sem, partner))
     arrived(pair, pair_sem)
-    half[...] = local[ds(core * rows, rows), :] + pair[...]
+    half[...] = local[at(core * rows, rows), :] + pair[...]
 
     for k, (q, dev) in enumerate(near_ids):
-        pending.append(send(half.at[ds(q * piece, piece)], near.at[me], near_out.at[k], near_sem.at[me], dev))
-    value = half[ds(me * piece, piece), :]
-    for q, _ in near_ids:
+        pending.append(send(half.at[at(8 * q)], near.at[me], near_out.at[k], near_sem.at[me], dev))
+    each_double(lambda k, dev: send(half.at[pl.ds(8 * (cell + k), 8)], more.at[me], more_out.at[k], more_sem.at[me], dev))
+    value = half[at(8 * me), :]
+    for q, _ in reversed(near_ids):
         arrived(near.at[q], near_sem.at[q])
         value = value + near[q]
-    mine[...] = value
-
-    for t, owner in enumerate(owners):
-        tile = pl.ds(8 * t, 8)
-
-        @pl.when(z != owner)
-        def _():
-            send(mine.at[tile], far.at[t, z], far_out.at[t], far_sem.at[t, z], ((owner * ny + y) * 2 + core, x))
-
-    for t, owner in enumerate(owners):
-        tile = pl.ds(8 * t, 8)
-
-        @pl.when(z == owner)
-        def _():
-            value = mine[8 * t:8 * t + 8, :]
-            for dz, qz, dev in far_ids:
-                arrived(far.at[t, qz], far_sem.at[t, qz])
-                value = value + far[t, qz]
-            total[8 * t:8 * t + 8, :] = value
-            for dz, qz, dev in far_ids:
-                send(total.at[tile], total.at[tile], total_out.at[t, dz], total_sem.at[t], dev)
-
-    for t, owner in enumerate(owners):
-        tile = pl.ds(8 * t, 8)
-
-        @pl.when(z != owner)
-        def _():
-            arrived(total.at[tile], total_sem.at[t])
-
-    slot = core * peers
+    mine[0:8, :] = value
+
+    @pl.when(jnp.logical_not(double))
+    def _():
+        for k, (q, dev) in enumerate(far_ids):
+            send(mine.at[0:8], far.at[step, 0:8], far_out.at[k], far_sem.at[step], dev)
+        far[step, 0:8] = mine[0:8, :]
+        for q, _ in reversed(far_ids):
+            arrived(far.at[q, 0:8], far_sem.at[q])
+        value = far[0, 0:8]
+        for k in range(1, steps):
+            value = value + far[k, 0:8]
+        total[0:8, :] = value
+
+    @pl.when(double)
+    def _():
+        value = half[at(8 * (cell + mine_second)), :]
+        for q, _ in reversed(near_ids):
+            arrived(more.at[q], more_sem.at[q])
+            value = value + more[q]
+        mine[8:16, :] = value
+        for k, (q, dev) in enumerate(far_ids):
+            send(mine, far.at[step], far_out.at[k], far_sem.at[step], dev)
+        far[step] = mine[...]
+        for q, _ in reversed(far_ids):
+            arrived(far.at[q], far_sem.at[q])
+        value = far[0]
+        for k in range(1, steps):
+            value = value + far[k]
+        total[...] = value
+
+    base = core * rows
     for k, (q, dev) in enumerate(near_ids):
-        pending.append(send(total, full.at[slot + me], back_out.at[k], back_sem.at[me], dev))
-    pending.append(send(total, full.at[slot + me], cross_out.at[me], cross_sem.at[me], partner))
-    full[slot + me] = total[...]
+        pending.append(send(total.at[0:8], full.at[at(base + 8 * me)], back_out.at[k], back_sem.at[me], dev))
+    pending.append(send(total.at[0:8], full.at[at(base + 8 * me)], cross_out.at[me], cross_sem.at[me], partner))
+    full[at(base + 8 * me), :] = total[0:8, :]
+
+    @pl.when(double)
+    def _():
+        spot = base + 8 * (cell + mine_second)
+        for k, (q, dev) in enumerate(near_ids):
+            send(total.at[8:16], full.at[at(spot)], rest_out.at[k], rest_sem.at[mine_second], dev)
+        full[at(spot), :] = total[8:16, :]
+
     for q, _ in reversed(near_ids):
-        arrived(full.at[slot + q], back_sem.at[q])
-        pending.append(send(full.at[slot + q], full.at[slot + q], cross_out.at[q], cross_sem.at[q], partner))
-    other = (1 - core) * peers
-    for q in range(peers):
-        arrived(full.at[other + q], cross_sem.at[q])
-    for q in range(2 * peers):
-        out_ref[q * piece:(q + 1) * piece, :] = full[q]
+        tile = full.at[at(base + 8 * q)]
+        arrived(tile, back_sem.at[q])
+        pending.append(send(tile, tile, cross_out.at[q], cross_sem.at[q], partner))
+
+    def rest_arrived(k, dev):
+        arrived(full.at[at(base + 8 * (cell + k))], rest_sem.at[k])
+
+    each_double(rest_arrived)
+    tail = full.at[at(base + 8 * cell, rows - 8 * cell)]
+    pending.append(send(tail, tail, cross_out.at[cell], cross_sem.at[cell], partner))
+    other = (1 - core) * rows
+    for q in range(cell):
+        arrived(full.at[at(other + 8 * q)], cross_sem.at[q])
+    arrived(full.at[at(other + 8 * cell, rows - 8 * cell)], cross_sem.at[cell])
+    out_ref[...] = full[...]
 
     for copy in pending:
         copy.wait_send()
-    for t, owner in enumerate(owners):
-        tile = pl.ds(8 * t, 8)
-
-        @pl.when(z != owner)
-        def _():
-            arrived(mine.at[tile], far_out.at[t])
-
-        @pl.when(z == owner)
-        def _():
-            for dz, _, _ in far_ids:
-                arrived(total.at[tile], total_out.at[t, dz])
+    each_double(lambda k, dev: arrived(half.at[pl.ds(8 * (cell + k), 8)], more_out.at[k]))
+
+    @pl.when(jnp.logical_not(double))
+    def _():
+        for k in range(len(far_ids)):
+            arrived(mine.at[0:8], far_out.at[k])
+
+    @pl.when(double)
+    def _():
+        for k in range(len(far_ids)):
+            arrived(mine, far_out.at[k])
+        for k in range(len(near_ids)):
+            arrived(total.at[8:16], rest_out.at[k])
 
 
 def reduce_all(sizes, a, b, v, d, r):
     nz, ny, nx = sizes
-    peers = ny * nx
-    piece = PACK // 2 // peers
-    tiles = piece // 8
+    cell, steps = 2 * ny * nx, nz // 2
+    rows = PACK // 2
+    twice = rows // 8 - cell
     vmem = pl.BlockSpec(memory_space=pltpu.VMEM)
     dma = pltpu.SemaphoreType.DMA
     return pl.pallas_call(
@@ -232,15 +268,16 @@
             *(pltpu.VMEM(value.shape, jnp.float32) for value in (a, b, v, d, r)),
             dma((5,)),
             pltpu.VMEM((PACK, LANES), jnp.float32),
-            pltpu.VMEM((PACK // 2, LANES), jnp.float32),
-            pltpu.VMEM((PACK // 2, LANES), jnp.float32),
-            pltpu.VMEM((peers, piece, LANES), jnp.float32),
-            pltpu.VMEM((piece, LANES), jnp.float32),
-            pltpu.VMEM((tiles, nz, 8, LANES), jnp.float32),
-            pltpu.VMEM((piece, LANES), jnp.float32),
-            pltpu.VMEM((2 * peers, piece, LANES), jnp.float32),
-            dma(()), dma((peers,)), dma((tiles, nz)), dma((tiles,)), dma((peers,)), dma((peers,)),
-            dma(()), dma((peers,)), dma((tiles,)), dma((tiles, nz)), dma((peers,)), dma((peers,)),
+            pltpu.VMEM((rows, LANES), jnp.float32),
+            pltpu.VMEM((rows, LANES), jnp.float32),
+            pltpu.VMEM((cell, 8, LANES), jnp.float32),
+            pltpu.VMEM((cell, 8, LANES), jnp.float32),
+            pltpu.VMEM((16, LANES), jnp.float32),
+            pltpu.VMEM((steps, 16, LANES), jnp.float32),
+            pltpu.VMEM((16, LANES), jnp.float32),
+            pltpu.VMEM((PACK, LANES), jnp.float32),
+            dma(()), dma((cell,)), dma((cell,)), dma((steps,)), dma((cell,)), dma((twice,)), dma((cell + 1,)),
+            dma(()), dma((cell,)), dma((twice,)), dma((steps,)), dma((cell,)), dma((cell,)), dma((cell + 1,)),
         ],
         compiler_params=pltpu.CompilerParams(collective_id=0, has_side_effects=True, vmem_limit_bytes=32 << 20),
     )(a, b, v, d, r)

time: 57.6 us -> 52.8 us (0.917)
  Pallas kernels: 56.8 us -> 52.1 us
    pallas_call x1, Pallas kernels: 44.9 us -> 40.1 us  [reduce_all(): pl.pallas_call(functools.partial(reduce_kernel, sizes), out_shape=jax.Sha...]
where the time goes in v4:
time: 52.8 us; the launch traced here: 52.7 us
  Pallas kernels  52.1 us (99%)
  between operations  0.64 us (1%)
    pallas_call x1, Pallas kernels, reduce_all(): pl.pallas_call(functools.partial(reduce_kernel, sizes), out_shape=jax.Sha...  40.1 us
    pallas_call x1, Pallas kernels, finish(): pl.pallas_call(chain_kernel, out_shape=(jax.ShapeDtypeStruct((1, rows), j...  12 us

profile of v4, /device:TPU:1, one launch (start us, length us, event | category | flops | bytes accessed | tf_op | source)
XLA Modules:
  0.0 52.7 jit_solution(10746955202502010485)
XLA Ops:
  0.6 40.1 %shard_map.76.red_ref = f32[704,128]{1,0:T(8,128)S(1)} custom-call(f32[256,256]{1,0:T(8,128)} %a_hbm.3, f32[256,256]{1,0:T(8,128)} %b_hbm.3, f32[32,256]{1,0:T(8,128)} %bitcast.4, f32[32,256]{1,0:T(8,128)} %bitcast.6, f32[1,256]{1,0:T(1,128)} %bitcast.8), custom_call_target="tpu_custom_call" | custom-call | tf_op jit(solution)/shard_map/pallas_call | solution.py:262
  40.7 12.0 %shard_map.77 = (f32[1,256]{1,0:T(1,128)}, f32[256,256]{1,0:T(8,128)}, f32[256,256]{1,0:T(8,128)}) custom-call(f32[704,128]{1,0:T(8,128)S(1)} %shard_map.76.red_ref, f32[256,256]{1,0:T(8,128)} %a_hbm.3, f32[256,256]{1,0:T(8,128)} %b_hbm.3, f32[32,256]{1,0:T(8,128)} %bitcast.5, f32[32,256]{1,0:T(8,128)} %bitcast.7), custom_call_target="tpu_custom_call" | custom-call | tf_op jit(solution)/shard_map/pallas_call | solution.py:415

commit v5 on v4

--- a/solution.py
+++ b/solution.py
@@ -283,31 +283,38 @@
     )(a, b, v, d, r)
 
 
-def inverse_factor(tile, lane_in, lane_out):
+def eliminate(tile, offset, carried):
     groups = BLOCK // 8
     sub = lax.broadcasted_iota(jnp.int32, (8, LANES), 0)
-    lane = lax.broadcasted_iota(jnp.int32, (8, LANES), 1)
     columns = [
         {
-            i: jnp.broadcast_to(tile[8 * i:8 * i + 8, lane_in + j:lane_in + j + 1], (8, LANES))
+            i: jnp.broadcast_to(tile[8 * i:8 * i + 8, offset + j:offset + j + 1], (8, LANES))
             for i in range(j // 8, groups)
         }
         for j in range(BLOCK)
     ]
-    out = [jnp.where(lane == sub + (8 * i + lane_out), 1.0, 0.0) for i in range(groups)]
+    carried = [[part[8 * i:8 * i + 8, :] for i in range(groups)] for part in carried]
     for j in range(BLOCK):
         g, r = j // 8, j % 8
         scale = lax.rsqrt(columns[j][g][r:r + 1, :])
         column = {i: columns[j][i] * scale for i in range(g, groups)}
-        pivot = out[g][r:r + 1, :] * scale
         for b in range(j + 1, BLOCK):
             factor = column[b // 8][b % 8:b % 8 + 1, :]
             for i in range(b // 8, groups):
                 columns[b][i] = columns[b][i] - column[i] * factor
-        out[g] = jnp.where(sub > r, out[g] - column[g] * pivot, jnp.where(sub == r, pivot, out[g]))
-        for i in range(g + 1, groups):
-            out[i] = out[i] - column[i] * pivot
-    return jnp.concatenate(out, axis=0)
+        below = jnp.where(sub > r, column[g], 0.0)
+        for out in carried:
+            pivot = out[g][r:r + 1, :] * scale
+            out[g] = jnp.where(sub == r, pivot, out[g] - below * pivot)
+            for i in range(g + 1, groups):
+                out[i] = out[i] - column[i] * pivot
+    return [jnp.concatenate(out, axis=0) for out in carried]
+
+
+def identity_at(offset):
+    row = lax.broadcasted_iota(jnp.int32, (BLOCK, LANES), 0)
+    lane = lax.broadcasted_iota(jnp.int32, (BLOCK, LANES), 1)
+    return jnp.where(lane == row + offset, 1.0, 0.0)
 
 
 def largest(values):
@@ -320,93 +327,112 @@
     return jnp.where(row == lane, matrix, 0.0)
 
 
-def framed(rows, before, after):
-    parts = [rows]
-    if before:
-        parts = [jnp.zeros((before, rows.shape[1]), rows.dtype)] + parts
-    if after:
-        parts = parts + [jnp.zeros((after, rows.shape[1]), rows.dtype)]
-    return jnp.concatenate(parts, axis=0) if len(parts) > 1 else rows
-
-
-def chain_kernel(red_ref, a_hbm, b_hbm, v_hbm, d_hbm, up_ref, na_ref, nb_ref, a_ref, b_ref, v_ref, d_ref, load_sem, z_ref, f_ref):
+def chain_kernel(red_ref, a_hbm, b_hbm, v_hbm, d_hbm, up_ref, na_ref, nb_ref, a_ref, b_ref, v_ref, d_ref, load_sem, z_ref, y_ref, x_ref):
     loads = fetch((a_hbm, b_hbm, v_hbm, d_hbm), (a_ref, b_ref, v_ref, d_ref), load_sem)
     rows, width = a_ref.shape
     cols = v_ref.shape[0]
     small = red_ref[656:696, :]
-    lower_inv = inverse_factor(small[:cols, :], 64, 0)[:, :cols]
-    inv_v = dot(lower_inv.T, lower_inv)
+    va = jnp.concatenate([red_ref[512:512 + cols, :], red_ref[512 + cols:576, :]], axis=1)
+    db = jnp.concatenate([red_ref[576:616, :], red_ref[616:656, :]], axis=1)
+    proj_t, proj_r = db[:cols, :], db[cols:cols + 8, :]
+    solved = eliminate(small[:cols, :], 64, [identity_at(0), proj_t[:, :LANES], proj_t[:, LANES:]])
+    low = solved[0][:, :cols]
+    low_t, low = halves(low.T), halves(low)
+    half = jnp.concatenate(solved[1:], axis=1)
+    half_t, half = halves(half.T), halves(half)
     vv = small[:cols, :cols]
     gram_r = small[cols:cols + 8, 64:64 + cols]
     gram_a = unpack_pair(red_ref, 0, red_ref[696:697, :])
     gram_b = unpack_pair(red_ref, 256, red_ref[697:698, :])
-    va = jnp.concatenate([red_ref[512:512 + cols, :], red_ref[512 + cols:576, :]], axis=1)
-    db = jnp.concatenate([red_ref[576:616, :], red_ref[616:656, :]], axis=1)
-    proj_t, proj_r = db[:cols, :], db[cols:cols + 8, :]
     scale_a = 1.0 / jnp.maximum(largest(diagonal(gram_a)), largest(diagonal(vv)))
     scale_b = 1.0 / largest(diagonal(gram_b))
-    gram_a = gram_a * scale_a
+    gram_a = halves(gram_a * scale_a)
     va = va * scale_a
-    vv = vv * scale_a
-    av = va.T
-    proj = proj_t.T
-
-    inv_v = halves(inv_v)
-    w = dot(inv_v, proj_t)
-    proj = halves(proj)
-    wt = dot(proj, inv_v)
+    vv = halves(vv * scale_a)
+    av, va = halves(va.T), halves(va)
+
+    s = halves((gram_b - dot(half_t, half)) * scale_b)
+    w = dot(low_t, half)
     ws = halves(w * scale_b)
-    wst = halves(wt * scale_b)
-    s = halves((gram_b - dot(proj, w)) * scale_b)
-    gram_a, va, vv, av = halves(gram_a), halves(va), halves(vv), halves(av)
+    wst = halves(dot(half_t, low) * scale_b)
+    inv_v = halves(dot(low_t, low))
     k1 = halves(dot(gram_a, s) + dot(av, ws))
-    k1t = dot(s, gram_a) + dot(wst, va)
+    k1t = halves(dot(s, gram_a) + dot(wst, va))
     k2 = dot(va, s) + dot(vv, ws)
-    k2t = dot(s, av) + dot(wst, vv)
+    k2t = halves(dot(s, av) + dot(wst, vv))
     j1 = halves(dot(s, k1))
     c = dot(inv_v, k2)
     cs = halves(c * scale_b)
-    z_ref[...] = dot(k1t, j1) + dot(k2t, cs)
-
-    for copy in loads:
-        copy.wait()
-    v, d = v_ref[...], d_ref[...]
-    coeffs = -dot(gram_r, inv_v)
-    lead = -proj_r - dot(coeffs, proj_t)
-    a = halves(a_ref[...])
-    up = dot(lead, a, NT) + dot(coeffs, v)
-    up_ref[...] = up[:1, :]
+
+    def rows_of(pair, start, stop):
+        return tuple(part[start:stop, :] for part in pair)
+
+    def lanes_of(pair, start):
+        return tuple(part[:, start:start + LANES] for part in pair)
+
+    z_ref[:LANES, :] = dot(rows_of(k1t, 0, LANES), j1) + dot(rows_of(k2t, 0, LANES), cs)
+    z_ref[LANES:, LANES:] = dot(rows_of(k1t, LANES, width), lanes_of(j1, LANES)) + dot(
+        rows_of(k2t, LANES, width), lanes_of(cs, LANES)
+    )
+    row = lax.broadcasted_iota(jnp.int32, (width, width), 0)
+    column = lax.broadcasted_iota(jnp.int32, (width, width), 1)
+    y_ref[...] = jnp.where(row == column, 1.0, 0.0)
+    lane = lax.broadcasted_iota(jnp.int32, (BLOCK, LANES), 1)
     root = jnp.sqrt(scale_b)
-    f_ref[:rows, :] = (dot(a, j1) + dot(v.T, cs)) / root
-    dn = halves(d.T)
-    f_ref[rows:, :] = (dot(b_ref[...] - dot(dn, w), k1) + dot(dn, c)) * root
+    fronts = []
 
     for lo in range(0, width, BLOCK):
         hi = lo + BLOCK
         base = lo // LANES * LANES
-        tile = slice(base, base + LANES)
-        inv = inverse_factor(z_ref[lo:hi, tile], lo - base, lo - base)
-        inv = halves(framed(inv, lo - base, base + LANES - hi))
+        own = slice(base, base + LANES)
+        offset = lo - base
+        block = z_ref[lo:hi, own]
+        inside = (lane >= offset) & (lane < offset + BLOCK)
+        carried = [jnp.where(inside, identity_at(offset), block)]
+        carried += [z_ref[lo:hi, start:start + LANES] for start in range(base + LANES, width, LANES)]
+        carried = eliminate(block, offset, carried)
+        inv = halves(jnp.where(inside, carried[0], 0.0))
+        right = {start: halves(part) for start, part in zip(range(base, width, LANES), carried) if start + LANES > hi}
+        left = {start: halves(part.T) for start, part in zip(range(base, width, LANES), carried) if start + LANES > hi}
         if hi < width:
-            panel = halves(dot(z_ref[hi:, tile], inv, NT))
-            for start in range(hi // LANES * LANES, width, LANES):
-                first = max(hi, start)
-                left = tuple(part[first - hi:, :] for part in panel)
-                right = tuple(framed(part[first - hi:start + LANES - hi, :], first - start, 0) for part in panel)
-                z_ref[first:, start:start + LANES] = z_ref[first:, start:start + LANES] - dot(left, right, NT)
-        done = dot(f_ref[:, tile], inv, NT)
-        if lo == base:
-            na_ref[:, tile] = done[:rows, :]
-            nb_ref[:, tile] = done[rows:, :]
-        else:
-            na_ref[:, tile] = na_ref[:, tile] + done[:rows, :]
-            nb_ref[:, tile] = nb_ref[:, tile] + done[rows:, :]
-        if hi < width:
-            done = halves(done)
-            for start in range(hi // LANES * LANES, width, LANES):
-                first = max(hi, start)
-                right = tuple(framed(part[first - hi:start + LANES - hi, :], first - start, 0) for part in panel)
-                f_ref[:, start:start + LANES] = f_ref[:, start:start + LANES] - dot(done, right, NT)
+            first = hi // LANES * LANES
+            near = rows_of(left[first], hi - first, hi - first + BLOCK)
+            for start in right:
+                tile = slice(start, start + LANES)
+                z_ref[hi:hi + BLOCK, tile] = z_ref[hi:hi + BLOCK, tile] - dot(near, right[start])
+        solved = dot(inv, y_ref[own, :base + LANES])
+        x_ref[lo:hi, :base + LANES] = solved
+        if base + LANES < width:
+            x_ref[lo:hi, base + LANES:] = jnp.zeros((BLOCK, width - base - LANES), jnp.float32)
+        solved = halves(solved)
+        for start in right:
+            top = max(hi, start)
+            part = rows_of(left[start], top - start, LANES)
+            y_ref[top:start + LANES, :base + LANES] = y_ref[top:start + LANES, :base + LANES] - dot(part, solved)
+            top = max(hi + BLOCK, start)
+            if top < start + LANES:
+                part = rows_of(left[start], top - start, LANES)
+                for other in right:
+                    if other >= start:
+                        tile = slice(other, other + LANES)
+                        z_ref[top:start + LANES, tile] = z_ref[top:start + LANES, tile] - dot(part, right[other])
+
+        if lo == 0:
+            for copy in loads:
+                copy.wait()
+            coeffs = -dot(gram_r, inv_v)
+            lead = -proj_r - dot(coeffs, proj_t)
+            a = halves(a_ref[...])
+            up = dot(lead, a, NT) + dot(coeffs, v_ref[...])
+            up_ref[...] = up[:1, :]
+            fronts.append(halves((dot(a, j1) + dot(v_ref[...].T, cs)) / root))
+        if lo == BLOCK:
+            d = halves(d_ref[...].T)
+            fronts.append(halves((dot(b_ref[...] - dot(d, w), k1) + dot(d, c)) * root))
+        if hi % LANES == 0:
+            back = halves(x_ref[own, :])
+            na_ref[:, own] = dot(fronts[0], back, NT)
+            nb_ref[:, own] = dot(fronts[1], back, NT)
 
 
 def finish(red, a, b, v, d):
@@ -424,7 +450,8 @@
         scratch_shapes=[
             *(pltpu.VMEM(value.shape, jnp.float32) for value in (a, b, v, d)),
             pltpu.SemaphoreType.DMA((4,)),
-            pltpu.VMEM((width, width), jnp.float32), pltpu.VMEM((2 * rows, width), jnp.float32)],
+            pltpu.VMEM((width, width), jnp.float32), pltpu.VMEM((width, width), jnp.float32),
+            pltpu.VMEM((width, width), jnp.float32)],
         compiler_params=pltpu.CompilerParams(vmem_limit_bytes=32 << 20),
     )(red, a, b, v, d)
 

time: 52.8 us -> 51.2 us (0.970)
  Pallas kernels: 52.1 us -> 50.4 us
    pallas_call x1, Pallas kernels: 12 us -> 10.3 us  [finish(): pl.pallas_call(chain_kernel, out_shape=(jax.ShapeDtypeStruct((1, rows), j...]
where the time goes in v5:
time: 51.2 us; the launch traced here: 51 us
  Pallas kernels  50.4 us (98%)
  between operations  0.64 us (1%)
    pallas_call x1, Pallas kernels, reduce_all(): pl.pallas_call(functools.partial(reduce_kernel, sizes), out_shape=jax.Sha...  40.1 us
    pallas_call x1, Pallas kernels, finish(): pl.pallas_call(chain_kernel, out_shape=(jax.ShapeDtypeStruct((1, rows), j...  10.3 us

profile of v5, /device:TPU:1, one launch (start us, length us, event | category | flops | bytes accessed | tf_op | source)
XLA Modules:
  0.0 51.0 jit_solution(11579557048732577863)
XLA Ops:
  0.6 40.1 %shard_map.76.red_ref = f32[704,128]{1,0:T(8,128)S(1)} custom-call(f32[256,256]{1,0:T(8,128)} %a_hbm.3, f32[256,256]{1,0:T(8,128)} %b_hbm.3, f32[32,256]{1,0:T(8,128)} %bitcast.4, f32[32,256]{1,0:T(8,128)} %bitcast.6, f32[1,256]{1,0:T(1,128)} %bitcast.8), custom_call_target="tpu_custom_call" | custom-call | tf_op jit(solution)/shard_map/pallas_call | solution.py:262
  40.7 10.3 %shard_map.77 = (f32[1,256]{1,0:T(1,128)}, f32[256,256]{1,0:T(8,128)}, f32[256,256]{1,0:T(8,128)}) custom-call(f32[704,128]{1,0:T(8,128)S(1)} %shard_map.76.red_ref, f32[256,256]{1,0:T(8,128)} %a_hbm.3, f32[256,256]{1,0:T(8,128)} %b_hbm.3, f32[32,256]{1,0:T(8,128)} %bitcast.5, f32[32,256]{1,0:T(8,128)} %bitcast.7), custom_call_target="tpu_custom_call" | custom-call | tf_op jit(solution)/shard_map/pallas_call | solution.py:441

commit v6 on v5

--- a/solution.py
+++ b/solution.py
@@ -94,7 +94,9 @@
                     hops = dz + min(dy, ny - dy) + min(dx, nx - dx)
                     dev = (((2 * step + qz) * ny + qy) * 2 + core, qx)
                     near_ids.append((hops, len(near_ids), qz * plane + qy * nx + qx, dev))
-    near_ids = [item[2:] for item in sorted(near_ids, key=lambda item: (-item[0], item[1]))]
+    near_ids = sorted(near_ids, key=lambda item: (-item[0], item[1]))
+    rings = [[(q, dev) for hops, _, q, dev in near_ids if hops == ring] for ring in range(1, near_ids[0][0] + 1)]
+    near_ids = [(hops - 1, q, dev) for hops, _, q, dev in near_ids]
     far_ids = []
     for dz in sorted(range(1, steps), key=lambda d: -min(d, steps - d)):
         qz = lax.rem(step + dz, steps)
@@ -110,7 +112,7 @@
     barrier = pltpu.get_barrier_semaphore()
     for _, dev in far_ids:
         pl.semaphore_signal(barrier, inc=1, device_id=dev, device_id_type=MESH)
-    for _, dev in near_ids:
+    for _, _, dev in near_ids:
         pl.semaphore_signal(barrier, inc=1, device_id=dev, device_id_type=MESH)
     pl.semaphore_signal(barrier, inc=1, device_id=partner, device_id_type=MESH)
 
@@ -142,19 +144,18 @@
     pl.semaphore_wait(barrier, len(far_ids) + len(near_ids) + 1)
 
     def send(src, dst, out_sem, in_sem, dev):
-        copy = pltpu.make_async_remote_copy(
+        pltpu.make_async_remote_copy(
             src_ref=src, dst_ref=dst, send_sem=out_sem, recv_sem=in_sem, device_id=dev, device_id_type=MESH
-        )
-        copy.start()
-        return copy
+        ).start()
 
     def arrived(ref, sem):
         pltpu.make_async_copy(ref, ref, sem).wait()
 
-    pending = []
-
     def at(start, size=8):
         return pl.ds(pl.multiple_of(start, 8), size)
+
+    def wait_tiles(count, sem):
+        arrived(full.at[pl.ds(0, 8 * count)], sem)
 
     def each_double(action):
         for k, (qz, qy, qx) in enumerate(doubles):
@@ -163,93 +164,91 @@
             def _():
                 action(k, (((2 * step + qz) * ny + qy) * 2 + core, qx))
 
-    pending.append(send(local.at[at((1 - core) * rows, rows)], pair, pair_out, pair_sem, partner))
+    others, lines = cell - 1, steps - 1
+    single = jnp.logical_not(double)
+
+    send(local.at[at((1 - core) * rows, rows)], pair, pair_out, pair_sem, partner)
     arrived(pair, pair_sem)
     half[...] = local[at(core * rows, rows), :] + pair[...]
 
-    for k, (q, dev) in enumerate(near_ids):
-        pending.append(send(half.at[at(8 * q)], near.at[me], near_out.at[k], near_sem.at[me], dev))
-    each_double(lambda k, dev: send(half.at[pl.ds(8 * (cell + k), 8)], more.at[me], more_out.at[k], more_sem.at[me], dev))
-    value = half[at(8 * me), :]
-    for q, _ in reversed(near_ids):
-        arrived(near.at[q], near_sem.at[q])
-        value = value + near[q]
-    mine[0:8, :] = value
-
-    @pl.when(jnp.logical_not(double))
-    def _():
-        for k, (q, dev) in enumerate(far_ids):
-            send(mine.at[0:8], far.at[step, 0:8], far_out.at[k], far_sem.at[step], dev)
+    for _, q, dev in near_ids:
+        send(half.at[at(8 * q)], near.at[me], near_out, near_sem, dev)
+    each_double(lambda k, dev: send(half.at[pl.ds(8 * (cell + k), 8)], more.at[me], more_out, more_sem, dev))
+    arrived(pair, pair_out)
+    near[me] = half[at(8 * me), :]
+    wait_tiles(others, near_sem)
+    mine[0:8, :] = jnp.sum(near[...], axis=0)
+
+    @pl.when(single)
+    def _():
+        for q, dev in far_ids:
+            send(mine.at[0:8], far.at[step, 0:8], far_out, far_sem, dev)
         far[step, 0:8] = mine[0:8, :]
-        for q, _ in reversed(far_ids):
-            arrived(far.at[q, 0:8], far_sem.at[q])
-        value = far[0, 0:8]
-        for k in range(1, steps):
-            value = value + far[k, 0:8]
-        total[0:8, :] = value
+        wait_tiles(others, near_out)
+        wait_tiles(len(doubles), more_out)
+        wait_tiles(lines, far_sem)
+        total[0:8, :] = jnp.sum(far[:, 0:8, :], axis=0)
 
     @pl.when(double)
     def _():
-        value = half[at(8 * (cell + mine_second)), :]
-        for q, _ in reversed(near_ids):
-            arrived(more.at[q], more_sem.at[q])
-            value = value + more[q]
-        mine[8:16, :] = value
-        for k, (q, dev) in enumerate(far_ids):
-            send(mine, far.at[step], far_out.at[k], far_sem.at[step], dev)
+        more[me] = half[at(8 * (cell + mine_second)), :]
+        wait_tiles(others, more_sem)
+        mine[8:16, :] = jnp.sum(more[...], axis=0)
+        for q, dev in far_ids:
+            send(mine, far.at[step], far_out, far_sem, dev)
         far[step] = mine[...]
-        for q, _ in reversed(far_ids):
-            arrived(far.at[q], far_sem.at[q])
-        value = far[0]
-        for k in range(1, steps):
-            value = value + far[k]
-        total[...] = value
+        wait_tiles(others, near_out)
+        wait_tiles(len(doubles) - 1, more_out)
+        wait_tiles(2 * lines, far_sem)
+        total[...] = jnp.sum(far[...], axis=0)
 
     base = core * rows
-    for k, (q, dev) in enumerate(near_ids):
-        pending.append(send(total.at[0:8], full.at[at(base + 8 * me)], back_out.at[k], back_sem.at[me], dev))
-    pending.append(send(total.at[0:8], full.at[at(base + 8 * me)], cross_out.at[me], cross_sem.at[me], partner))
+    for ring, q, dev in near_ids:
+        send(total.at[0:8], full.at[at(base + 8 * me)], back_out, back_sem.at[ring], dev)
+    send(total.at[0:8], full.at[at(base + 8 * me)], cross_out, cross_sem, partner)
     full[at(base + 8 * me), :] = total[0:8, :]
 
     @pl.when(double)
     def _():
         spot = base + 8 * (cell + mine_second)
-        for k, (q, dev) in enumerate(near_ids):
-            send(total.at[8:16], full.at[at(spot)], rest_out.at[k], rest_sem.at[mine_second], dev)
+        for _, q, dev in near_ids:
+            send(total.at[8:16], full.at[at(spot)], rest_out, rest_sem, dev)
+        send(total.at[8:16], full.at[at(spot)], cross_out, cross_sem, partner)
         full[at(spot), :] = total[8:16, :]
-
-    for q, _ in reversed(near_ids):
-        tile = full.at[at(base + 8 * q)]
-        arrived(tile, back_sem.at[q])
-        pending.append(send(tile, tile, cross_out.at[q], cross_sem.at[q], partner))
-
-    def rest_arrived(k, dev):
-        arrived(full.at[at(base + 8 * (cell + k))], rest_sem.at[k])
-
-    each_double(rest_arrived)
-    tail = full.at[at(base + 8 * cell, rows - 8 * cell)]
-    pending.append(send(tail, tail, cross_out.at[cell], cross_sem.at[cell], partner))
-    other = (1 - core) * rows
-    for q in range(cell):
-        arrived(full.at[at(other + 8 * q)], cross_sem.at[q])
-    arrived(full.at[at(other + 8 * cell, rows - 8 * cell)], cross_sem.at[cell])
+        wait_tiles(2 * lines, far_out)
+
+    @pl.when(single)
+    def _():
+        wait_tiles(lines, far_out)
+
+    for ring, members in enumerate(rings):
+        wait_tiles(len(members), back_sem.at[ring])
+        for q, dev in members:
+            tile = full.at[at(base + 8 * q)]
+            send(tile, tile, cross_out, cross_sem, partner)
+
+    @pl.when(single)
+    def _():
+        wait_tiles(len(doubles), rest_sem)
+
+    @pl.when(double)
+    def _():
+        wait_tiles(len(doubles) - 1, rest_sem)
+
+    def forward(k, dev):
+        tile = full.at[at(base + 8 * (cell + k))]
+        send(tile, tile, cross_out, cross_sem, partner)
+
+    each_double(forward)
+    wait_tiles(others, back_out)
+
+    @pl.when(double)
+    def _():
+        wait_tiles(others, rest_out)
+
+    arrived(full.at[at((1 - core) * rows, rows)], cross_sem)
+    arrived(full.at[at(base, rows)], cross_out)
     out_ref[...] = full[...]
-
-    for copy in pending:
-        copy.wait_send()
-    each_double(lambda k, dev: arrived(half.at[pl.ds(8 * (cell + k), 8)], more_out.at[k]))
-
-    @pl.when(jnp.logical_not(double))
-    def _():
-        for k in range(len(far_ids)):
-            arrived(mine.at[0:8], far_out.at[k])
-
-    @pl.when(double)
-    def _():
-        for k in range(len(far_ids)):
-            arrived(mine, far_out.at[k])
-        for k in range(len(near_ids)):
-            arrived(total.at[8:16], rest_out.at[k])
 
 
 def reduce_all(sizes, a, b, v, d, r):
@@ -276,8 +275,8 @@
             pltpu.VMEM((steps, 16, LANES), jnp.float32),
             pltpu.VMEM((16, LANES), jnp.float32),
             pltpu.VMEM((PACK, LANES), jnp.float32),
-            dma(()), dma((cell,)), dma((cell,)), dma((steps,)), dma((cell,)), dma((twice,)), dma((cell + 1,)),
-            dma(()), dma((cell,)), dma((twice,)), dma((steps,)), dma((cell,)), dma((cell,)), dma((cell + 1,)),
+            dma(()), dma(()), dma(()), dma(()), dma((8,)), dma(()), dma(()),
+            *(dma(()) for _ in range(7)),
         ],
         compiler_params=pltpu.CompilerParams(collective_id=0, has_side_effects=True, vmem_limit_bytes=32 << 20),
     )(a, b, v, d, r)
@@ -356,8 +355,8 @@
     ws = halves(w * scale_b)
     wst = halves(dot(half_t, low) * scale_b)
     inv_v = halves(dot(low_t, low))
-    k1 = halves(dot(gram_a, s) + dot(av, ws))
-    k1t = halves(dot(s, gram_a) + dot(wst, va))
+    k1 = dot(gram_a, s) + dot(av, ws)
+    k1t, k1 = halves(k1.T), halves(k1)
     k2 = dot(va, s) + dot(vv, ws)
     k2t = halves(dot(s, av) + dot(wst, vv))
     j1 = halves(dot(s, k1))

time: 51.2 us -> 48.4 us (0.945)
  Pallas kernels: 50.4 us -> 47.6 us
    pallas_call x1, Pallas kernels: 40.1 us -> 37.4 us  [reduce_all(): pl.pallas_call(functools.partial(reduce_kernel, sizes), out_shape=jax.Sha...]
where the time goes in v6:
time: 48.4 us; the launch traced here: 48.3 us
  Pallas kernels  47.6 us (98%)
  between operations  0.64 us (1%)
    pallas_call x1, Pallas kernels, reduce_all(): pl.pallas_call(functools.partial(reduce_kernel, sizes), out_shape=jax.Sha...  37.4 us
    pallas_call x1, Pallas kernels, finish(): pl.pallas_call(chain_kernel, out_shape=(jax.ShapeDtypeStruct((1, rows), j...  10.2 us

profile of v6, /device:TPU:1, one launch (start us, length us, event | category | flops | bytes accessed | tf_op | source)
XLA Modules:
  0.0 48.3 jit_solution(5875618009005408153)
XLA Ops:
  0.6 37.4 %shard_map.76.red_ref = f32[704,128]{1,0:T(8,128)S(1)} custom-call(f32[256,256]{1,0:T(8,128)} %a_hbm.3, f32[256,256]{1,0:T(8,128)} %b_hbm.3, f32[32,256]{1,0:T(8,128)} %bitcast.4, f32[32,256]{1,0:T(8,128)} %bitcast.6, f32[1,256]{1,0:T(1,128)} %bitcast.8), custom_call_target="tpu_custom_call" | custom-call | tf_op jit(solution)/shard_map/pallas_call | solution.py:261
  38.0 10.2 %shard_map.77 = (f32[1,256]{1,0:T(1,128)}, f32[256,256]{1,0:T(8,128)}, f32[256,256]{1,0:T(8,128)}) custom-call(f32[704,128]{1,0:T(8,128)S(1)} %shard_map.76.red_ref, f32[256,256]{1,0:T(8,128)} %a_hbm.3, f32[256,256]{1,0:T(8,128)} %b_hbm.3, f32[32,256]{1,0:T(8,128)} %bitcast.5, f32[32,256]{1,0:T(8,128)} %bitcast.7), custom_call_target="tpu_custom_call" | custom-call | tf_op jit(solution)/shard_map/pallas_call | solution.py:440

commit v7 on v6

--- a/solution.py
+++ b/solution.py
@@ -11,6 +11,7 @@
 LANES = 128
 PACK = 704
 BLOCK = 32
+NEXT = 4
 
 NN = (((1,), (0,)), ((), ()))
 NT = (((1,), (1,)), ((), ()))
@@ -282,7 +283,7 @@
     )(a, b, v, d, r)
 
 
-def eliminate(tile, offset, carried):
+def eliminate(tile, offset, carried, spread):
     groups = BLOCK // 8
     sub = lax.broadcasted_iota(jnp.int32, (8, LANES), 0)
     columns = [
@@ -297,8 +298,13 @@
         g, r = j // 8, j % 8
         scale = lax.rsqrt(columns[j][g][r:r + 1, :])
         column = {i: columns[j][i] * scale for i in range(g, groups)}
+        for i in range(g, groups):
+            spread[j, 8 * i:8 * i + 8, :] = column[i]
         for b in range(j + 1, BLOCK):
-            factor = column[b // 8][b % 8:b % 8 + 1, :]
+            if b < j + NEXT:
+                factor = column[b // 8][b % 8:b % 8 + 1, :]
+            else:
+                factor = spread[j, b:b + 1, :]
             for i in range(b // 8, groups):
                 columns[b][i] = columns[b][i] - column[i] * factor
         below = jnp.where(sub > r, column[g], 0.0)
@@ -326,7 +332,7 @@
     return jnp.where(row == lane, matrix, 0.0)
 
 
-def chain_kernel(red_ref, a_hbm, b_hbm, v_hbm, d_hbm, up_ref, na_ref, nb_ref, a_ref, b_ref, v_ref, d_ref, load_sem, z_ref, y_ref, x_ref):
+def chain_kernel(red_ref, a_hbm, b_hbm, v_hbm, d_hbm, up_ref, na_ref, nb_ref, a_ref, b_ref, v_ref, d_ref, load_sem, z_ref, y_ref, x_ref, spread):
     loads = fetch((a_hbm, b_hbm, v_hbm, d_hbm), (a_ref, b_ref, v_ref, d_ref), load_sem)
     rows, width = a_ref.shape
     cols = v_ref.shape[0]
@@ -334,7 +340,7 @@
     va = jnp.concatenate([red_ref[512:512 + cols, :], red_ref[512 + cols:576, :]], axis=1)
     db = jnp.concatenate([red_ref[576:616, :], red_ref[616:656, :]], axis=1)
     proj_t, proj_r = db[:cols, :], db[cols:cols + 8, :]
-    solved = eliminate(small[:cols, :], 64, [identity_at(0), proj_t[:, :LANES], proj_t[:, LANES:]])
+    solved = eliminate(small[:cols, :], 64, [identity_at(0), proj_t[:, :LANES], proj_t[:, LANES:]], spread)
     low = solved[0][:, :cols]
     low_t, low = halves(low.T), halves(low)
     half = jnp.concatenate(solved[1:], axis=1)
@@ -388,9 +394,14 @@
         block = z_ref[lo:hi, own]
         inside = (lane >= offset) & (lane < offset + BLOCK)
         carried = [jnp.where(inside, identity_at(offset), block)]
-        carried += [z_ref[lo:hi, start:start + LANES] for start in range(base + LANES, width, LANES)]
-        carried = eliminate(block, offset, carried)
+        rest = [z_ref[lo:hi, start:start + LANES] for start in range(base + LANES, width, LANES)]
+        if hi % LANES == 0:
+            carried += rest
+        carried = eliminate(block, offset, carried, spread)
         inv = halves(jnp.where(inside, carried[0], 0.0))
+        if hi % LANES:
+            narrow = halves(pltpu.roll(jnp.where(inside, carried[0], 0.0), (LANES - offset) % LANES, 1)[:, :BLOCK])
+            carried += [dot(narrow, part) for part in rest]
         right = {start: halves(part) for start, part in zip(range(base, width, LANES), carried) if start + LANES > hi}
         left = {start: halves(part.T) for start, part in zip(range(base, width, LANES), carried) if start + LANES > hi}
         if hi < width:
@@ -450,7 +461,7 @@
             *(pltpu.VMEM(value.shape, jnp.float32) for value in (a, b, v, d)),
             pltpu.SemaphoreType.DMA((4,)),
             pltpu.VMEM((width, width), jnp.float32), pltpu.VMEM((width, width), jnp.float32),
-            pltpu.VMEM((width, width), jnp.float32)],
+            pltpu.VMEM((width, width), jnp.float32), pltpu.VMEM((BLOCK, BLOCK, LANES), jnp.float32)],
         compiler_params=pltpu.CompilerParams(vmem_limit_bytes=32 << 20),
     )(red, a, b, v, d)
 

time: 48.4 us -> 48.1 us (level)
  no operation moved by 1% of the time
where the time goes in v7:
time: 48.1 us; the launch traced here: 48 us
  Pallas kernels  47.3 us (98%)
  between operations  0.64 us (1%)
    pallas_call x1, Pallas kernels, reduce_all(): pl.pallas_call(functools.partial(reduce_kernel, sizes), out_shape=jax.Sha...  37.4 us
    pallas_call x1, Pallas kernels, finish(): pl.pallas_call(chain_kernel, out_shape=(jax.ShapeDtypeStruct((1, rows), j...  9.94 us

profile of v7, /device:TPU:1, one launch (start us, length us, event | category | flops | bytes accessed | tf_op | source)
XLA Modules:
  0.0 48.0 jit_solution(6167452487300478679)
XLA Ops:
  0.6 37.4 %shard_map.76.red_ref = f32[704,128]{1,0:T(8,128)S(1)} custom-call(f32[256,256]{1,0:T(8,128)} %a_hbm.3, f32[256,256]{1,0:T(8,128)} %b_hbm.3, f32[32,256]{1,0:T(8,128)} %bitcast.4, f32[32,256]{1,0:T(8,128)} %bitcast.6, f32[1,256]{1,0:T(1,128)} %bitcast.8), custom_call_target="tpu_custom_call" | custom-call | tf_op jit(solution)/shard_map/pallas_call | solution.py:262
  38.0 9.9 %shard_map.77 = (f32[1,256]{1,0:T(1,128)}, f32[256,256]{1,0:T(8,128)}, f32[256,256]{1,0:T(8,128)}) custom-call(f32[704,128]{1,0:T(8,128)S(1)} %shard_map.76.red_ref, f32[256,256]{1,0:T(8,128)} %a_hbm.3, f32[256,256]{1,0:T(8,128)} %b_hbm.3, f32[32,256]{1,0:T(8,128)} %bitcast.5, f32[32,256]{1,0:T(8,128)} %bitcast.7), custom_call_target="tpu_custom_call" | custom-call | tf_op jit(solution)/shard_map/pallas_call | solution.py:451

commit v8 on v7

--- a/solution.py
+++ b/solution.py
@@ -118,31 +118,33 @@
     pl.semaphore_signal(barrier, inc=1, device_id=partner, device_id_type=MESH)
 
     cols = v_ref.shape[0]
-    for copy in loads[:3]:
-        copy.wait()
-    diag_b = gram_pair(b_ref[...], local, 2 * LANES)
-    d = d_ref[...]
-    left = halves(jnp.concatenate([d, jnp.broadcast_to(r_ref[...], (8, d.shape[1]))], axis=0))
-    db = dot(left, b_ref[...])
-    dd = dot(left, d, NT)
-    for copy in loads[3:]:
-        copy.wait()
-    diag_a = gram_pair(a_ref[...], local, 0)
-    v = halves(v_ref[...])
-    va = dot(v, a_ref[...])
-    vv = dot(v, v, NT)
-    local[512:512 + cols, :] = va[:, :LANES]
-    local[512 + cols:576, :] = va[:, LANES:]
-    local[576:616, :] = db[:, :LANES]
-    local[616:656, :] = db[:, LANES:]
-    local[656:696, :] = jnp.zeros((40, LANES), jnp.float32)
-    local[656:656 + cols, 0:cols] = vv
-    local[656:696, 64:64 + cols] = dd
-    local[696:704, :] = jnp.zeros((8, LANES), jnp.float32)
-    local[696:697, :] = diag_a
-    local[697:698, :] = diag_b
-
-    pl.semaphore_wait(barrier, len(far_ids) + len(near_ids) + 1)
+
+    def half_a():
+        for k in (3, 4):
+            loads[k].wait()
+        diag = gram_pair(a_ref[...], local, 0)
+        v, d = halves(v_ref[...]), halves(d_ref[...])
+        va = dot(v, a_ref[...])
+        local[256:256 + cols, :] = va[:, :LANES]
+        local[256 + cols:320, :] = va[:, LANES:]
+        local[320:352, :] = jnp.zeros((32, LANES), jnp.float32)
+        local[320:320 + cols, 0:cols] = dot(v, v, NT)
+        local[320:320 + cols, 64:64 + cols] = dot(d, d, NT)
+        for k in range(4):
+            local[320 + k:321 + k, 32:64] = diag[:, 32 * k:32 * k + 32]
+
+    def half_b():
+        for k in (0, 2):
+            loads[k].wait()
+        diag = gram_pair(b_ref[...], local, rows)
+        d = d_ref[...]
+        last = jnp.broadcast_to(r_ref[...], (8, d.shape[1]))
+        db = dot(jnp.concatenate([d, last], axis=0), b_ref[...])
+        local[608:648, :] = db[:, :LANES]
+        local[648:688, :] = db[:, LANES:]
+        local[688:704, :] = jnp.zeros((16, LANES), jnp.float32)
+        local[688:689, :] = diag
+        local[696:704, 0:cols] = dot(last, d, NT)
 
     def send(src, dst, out_sem, in_sem, dev):
         pltpu.make_async_remote_copy(
@@ -168,7 +170,22 @@
     others, lines = cell - 1, steps - 1
     single = jnp.logical_not(double)
 
-    send(local.at[at((1 - core) * rows, rows)], pair, pair_out, pair_sem, partner)
+    @pl.when(core == 0)
+    def _():
+        loads[1].wait()
+        half_b()
+        pl.semaphore_wait(barrier, len(far_ids) + len(near_ids) + 1)
+        send(local.at[rows:PACK], pair, pair_out, pair_sem, partner)
+        half_a()
+
+    @pl.when(core == 1)
+    def _():
+        loads[1].wait()
+        half_a()
+        pl.semaphore_wait(barrier, len(far_ids) + len(near_ids) + 1)
+        send(local.at[0:rows], pair, pair_out, pair_sem, partner)
+        half_b()
+
     arrived(pair, pair_sem)
     half[...] = local[at(core * rows, rows), :] + pair[...]
 
@@ -336,9 +353,9 @@
     loads = fetch((a_hbm, b_hbm, v_hbm, d_hbm), (a_ref, b_ref, v_ref, d_ref), load_sem)
     rows, width = a_ref.shape
     cols = v_ref.shape[0]
-    small = red_ref[656:696, :]
-    va = jnp.concatenate([red_ref[512:512 + cols, :], red_ref[512 + cols:576, :]], axis=1)
-    db = jnp.concatenate([red_ref[576:616, :], red_ref[616:656, :]], axis=1)
+    small = red_ref[320:352, :]
+    va = jnp.concatenate([red_ref[256:256 + cols, :], red_ref[256 + cols:320, :]], axis=1)
+    db = jnp.concatenate([red_ref[608:648, :], red_ref[648:688, :]], axis=1)
     proj_t, proj_r = db[:cols, :], db[cols:cols + 8, :]
     solved = eliminate(small[:cols, :], 64, [identity_at(0), proj_t[:, :LANES], proj_t[:, LANES:]], spread)
     low = solved[0][:, :cols]
@@ -346,9 +363,10 @@
     half = jnp.concatenate(solved[1:], axis=1)
     half_t, half = halves(half.T), halves(half)
     vv = small[:cols, :cols]
-    gram_r = small[cols:cols + 8, 64:64 + cols]
-    gram_a = unpack_pair(red_ref, 0, red_ref[696:697, :])
-    gram_b = unpack_pair(red_ref, 256, red_ref[697:698, :])
+    gram_r = red_ref[696:704, :cols]
+    diag_a = jnp.concatenate([small[k:k + 1, 32:64] for k in range(4)], axis=1)
+    gram_a = unpack_pair(red_ref, 0, diag_a)
+    gram_b = unpack_pair(red_ref, 352, red_ref[688:689, :])
     scale_a = 1.0 / jnp.maximum(largest(diagonal(gram_a)), largest(diagonal(vv)))
     scale_b = 1.0 / largest(diagonal(gram_b))
     gram_a = halves(gram_a * scale_a)

time: 48.1 us -> 48.1 us (level)
  no operation moved by 1% of the time
where the time goes in v8:
time: 48.1 us; the launch traced here: 48 us
  Pallas kernels  47.4 us (99%)
  between operations  0.64 us (1%)
    pallas_call x1, Pallas kernels, reduce_all(): pl.pallas_call(functools.partial(reduce_kernel, sizes), out_shape=jax.Sha...  37.4 us
    pallas_call x1, Pallas kernels, finish(): pl.pallas_call(chain_kernel, out_shape=(jax.ShapeDtypeStruct((1, rows), j...  9.97 us

profile of v8, /device:TPU:1, one launch (start us, length us, event | category | flops | bytes accessed | tf_op | source)
XLA Modules:
  0.0 48.0 jit_solution(7199745114885083170)
XLA Ops:
  0.6 37.4 %shard_map.76.red_ref = f32[704,128]{1,0:T(8,128)S(1)} custom-call(f32[256,256]{1,0:T(8,128)} %a_hbm.3, f32[256,256]{1,0:T(8,128)} %b_hbm.3, f32[32,256]{1,0:T(8,128)} %bitcast.4, f32[32,256]{1,0:T(8,128)} %bitcast.6, f32[1,256]{1,0:T(1,128)} %bitcast.8), custom_call_target="tpu_custom_call" | custom-call | tf_op jit(solution)/shard_map/pallas_call | solution.py:279
  38.0 10.0 %shard_map.77 = (f32[1,256]{1,0:T(1,128)}, f32[256,256]{1,0:T(8,128)}, f32[256,256]{1,0:T(8,128)}) custom-call(f32[704,128]{1,0:T(8,128)S(1)} %shard_map.76.red_ref, f32[256,256]{1,0:T(8,128)} %a_hbm.3, f32[256,256]{1,0:T(8,128)} %b_hbm.3, f32[32,256]{1,0:T(8,128)} %bitcast.5, f32[32,256]{1,0:T(8,128)} %bitcast.7), custom_call_target="tpu_custom_call" | custom-call | tf_op jit(solution)/shard_map/pallas_call | solution.py:469

commit v9 on v8

--- a/solution.py
+++ b/solution.py
@@ -72,7 +72,7 @@
 
 def reduce_kernel(sizes, a_hbm, b_hbm, v_hbm, d_hbm, r_hbm, out_ref, a_ref, b_ref, v_ref, d_ref, r_ref, load_sem,
                   local, pair, half, near, more, mine, far, total, full,
-                  pair_sem, near_sem, more_sem, far_sem, back_sem, rest_sem, cross_sem,
+                  hello, pair_sem, near_sem, more_sem, far_sem, back_sem, rest_sem, cross_sem,
                   pair_out, near_out, more_out, far_out, back_out, rest_out, cross_out):
     nz, ny, nx = sizes
     rows = PACK // 2
@@ -103,6 +103,10 @@
         qz = lax.rem(step + dz, steps)
         far_ids.append((qz, ((2 * (2 * ny) * qz + 2 * ny * side) + 2 * y + core, x)))
     partner = (place + 1 - 2 * core, x)
+    beside = []
+    for dz in (1, steps - 1):
+        qz = lax.rem(step + dz, steps)
+        beside.append(((2 * (2 * ny) * qz + 2 * ny * side) + 2 * y + core, x))
     doubles = [(0, qy, qx) for qy in range(ny) for qx in range(nx) if (qx + qy) % 2 == 0]
     doubles += [(1, qy, qx) for qy in range(ny) for qx in range(nx) if (qx + qy) % 4 == 1]
     even = side == 0
@@ -111,7 +115,7 @@
 
     loads = fetch((b_hbm, d_hbm, r_hbm, a_hbm, v_hbm), (b_ref, d_ref, r_ref, a_ref, v_ref), load_sem)
     barrier = pltpu.get_barrier_semaphore()
-    for _, dev in far_ids:
+    for dev in beside:
         pl.semaphore_signal(barrier, inc=1, device_id=dev, device_id_type=MESH)
     for _, _, dev in near_ids:
         pl.semaphore_signal(barrier, inc=1, device_id=dev, device_id_type=MESH)
@@ -167,6 +171,13 @@
             def _():
                 action(k, (((2 * step + qz) * ny + qy) * 2 + core, qx))
 
+    def tell(level):
+        for dev in beside:
+            pl.semaphore_signal(hello.at[level], inc=1, device_id=dev, device_id_type=MESH)
+
+    def told(level):
+        pl.semaphore_wait(hello.at[level], 2)
+
     others, lines = cell - 1, steps - 1
     single = jnp.logical_not(double)
 
@@ -174,16 +185,18 @@
     def _():
         loads[1].wait()
         half_b()
-        pl.semaphore_wait(barrier, len(far_ids) + len(near_ids) + 1)
+        pl.semaphore_wait(barrier, len(beside) + len(near_ids) + 1)
         send(local.at[rows:PACK], pair, pair_out, pair_sem, partner)
+        tell(0)
         half_a()
 
     @pl.when(core == 1)
     def _():
         loads[1].wait()
         half_a()
-        pl.semaphore_wait(barrier, len(far_ids) + len(near_ids) + 1)
+        pl.semaphore_wait(barrier, len(beside) + len(near_ids) + 1)
         send(local.at[0:rows], pair, pair_out, pair_sem, partner)
+        tell(0)
         half_b()
 
     arrived(pair, pair_sem)
@@ -192,6 +205,10 @@
     for _, q, dev in near_ids:
         send(half.at[at(8 * q)], near.at[me], near_out, near_sem, dev)
     each_double(lambda k, dev: send(half.at[pl.ds(8 * (cell + k), 8)], more.at[me], more_out, more_sem, dev))
+    for level in range(steps // 2 - 1):
+        told(level)
+        if level < steps // 2 - 2:
+            tell(level + 1)
     arrived(pair, pair_out)
     near[me] = half[at(8 * me), :]
     wait_tiles(others, near_sem)
@@ -293,6 +310,7 @@
             pltpu.VMEM((steps, 16, LANES), jnp.float32),
             pltpu.VMEM((16, LANES), jnp.float32),
             pltpu.VMEM((PACK, LANES), jnp.float32),
+            pltpu.SemaphoreType.REGULAR((steps // 2 - 1,)),
             dma(()), dma(()), dma(()), dma(()), dma((8,)), dma(()), dma(()),
             *(dma(()) for _ in range(7)),
         ],

time: 48.1 us -> 48.1 us (level)
  no operation moved by 1% of the time
where the time goes in v9:
time: 48.1 us; the launch traced here: 48 us
  Pallas kernels  47.3 us (98%)
  between operations  0.64 us (1%)
    pallas_call x1, Pallas kernels, reduce_all(): pl.pallas_call(functools.partial(reduce_kernel, sizes), out_shape=jax.Sha...  37.4 us
    pallas_call x1, Pallas kernels, finish(): pl.pallas_call(chain_kernel, out_shape=(jax.ShapeDtypeStruct((1, rows), j...  9.97 us

profile of v9, /device:TPU:1, one launch (start us, length us, event | category | flops | bytes accessed | tf_op | source)
XLA Modules:
  0.0 48.0 jit_solution(13947509737092562139)
XLA Ops:
  0.6 37.4 %shard_map.76.red_ref = f32[704,128]{1,0:T(8,128)S(1)} custom-call(f32[256,256]{1,0:T(8,128)} %a_hbm.3, f32[256,256]{1,0:T(8,128)} %b_hbm.3, f32[32,256]{1,0:T(8,128)} %bitcast.4, f32[32,256]{1,0:T(8,128)} %bitcast.6, f32[1,256]{1,0:T(1,128)} %bitcast.8), custom_call_target="tpu_custom_call" | custom-call | tf_op jit(solution)/shard_map/pallas_call | solution.py:296
  38.0 10.0 %shard_map.77 = (f32[1,256]{1,0:T(1,128)}, f32[256,256]{1,0:T(8,128)}, f32[256,256]{1,0:T(8,128)}) custom-call(f32[704,128]{1,0:T(8,128)S(1)} %shard_map.76.red_ref, f32[256,256]{1,0:T(8,128)} %a_hbm.3, f32[256,256]{1,0:T(8,128)} %b_hbm.3, f32[32,256]{1,0:T(8,128)} %bitcast.5, f32[32,256]{1,0:T(8,128)} %bitcast.7), custom_call_target="tpu_custom_call" | custom-call | tf_op jit(solution)/shard_map/pallas_call | solution.py:487

commit v10 on v9

--- a/solution.py
+++ b/solution.py
@@ -11,7 +11,7 @@
 LANES = 128
 PACK = 704
 BLOCK = 32
-NEXT = 4
+NEXT = 2
 
 NN = (((1,), (0,)), ((), ()))
 NT = (((1,), (1,)), ((), ()))
@@ -331,20 +331,20 @@
     carried = [[part[8 * i:8 * i + 8, :] for i in range(groups)] for part in carried]
     for j in range(BLOCK):
         g, r = j // 8, j % 8
-        scale = lax.rsqrt(columns[j][g][r:r + 1, :])
+        scale = lax.rsqrt(jnp.broadcast_to(columns[j][g][r:r + 1, :], (8, LANES)))
         column = {i: columns[j][i] * scale for i in range(g, groups)}
         for i in range(g, groups):
             spread[j, 8 * i:8 * i + 8, :] = column[i]
         for b in range(j + 1, BLOCK):
             if b < j + NEXT:
-                factor = column[b // 8][b % 8:b % 8 + 1, :]
+                factor = jnp.broadcast_to(columns[j][b // 8][b % 8:b % 8 + 1, :], (8, LANES)) * scale
             else:
                 factor = spread[j, b:b + 1, :]
             for i in range(b // 8, groups):
                 columns[b][i] = columns[b][i] - column[i] * factor
         below = jnp.where(sub > r, column[g], 0.0)
         for out in carried:
-            pivot = out[g][r:r + 1, :] * scale
+            pivot = jnp.broadcast_to(out[g][r:r + 1, :], (8, LANES)) * scale
             out[g] = jnp.where(sub == r, pivot, out[g] - below * pivot)
             for i in range(g + 1, groups):
                 out[i] = out[i] - column[i] * pivot

time: 48.1 us -> 48.3 us (level)
  no operation moved by 1% of the time
where the time goes in v10:
time: 48.3 us; the launch traced here: 48.1 us
  Pallas kernels  47.5 us (98%)
  between operations  0.64 us (1%)
    pallas_call x1, Pallas kernels, reduce_all(): pl.pallas_call(functools.partial(reduce_kernel, sizes), out_shape=jax.Sha...  37.4 us
    pallas_call x1, Pallas kernels, finish(): pl.pallas_call(chain_kernel, out_shape=(jax.ShapeDtypeStruct((1, rows), j...  10.1 us

profile of v10, /device:TPU:1, one launch (start us, length us, event | category | flops | bytes accessed | tf_op | source)
XLA Modules:
  0.0 48.1 jit_solution(2262712153202305996)
XLA Ops:
  0.6 37.4 %shard_map.76.red_ref = f32[704,128]{1,0:T(8,128)S(1)} custom-call(f32[256,256]{1,0:T(8,128)} %a_hbm.3, f32[256,256]{1,0:T(8,128)} %b_hbm.3, f32[32,256]{1,0:T(8,128)} %bitcast.4, f32[32,256]{1,0:T(8,128)} %bitcast.6, f32[1,256]{1,0:T(1,128)} %bitcast.8), custom_call_target="tpu_custom_call" | custom-call | tf_op jit(solution)/shard_map/pallas_call | solution.py:296
  38.0 10.1 %shard_map.77 = (f32[1,256]{1,0:T(1,128)}, f32[256,256]{1,0:T(8,128)}, f32[256,256]{1,0:T(8,128)}) custom-call(f32[704,128]{1,0:T(8,128)S(1)} %shard_map.76.red_ref, f32[256,256]{1,0:T(8,128)} %a_hbm.3, f32[256,256]{1,0:T(8,128)} %b_hbm.3, f32[32,256]{1,0:T(8,128)} %bitcast.5, f32[32,256]{1,0:T(8,128)} %bitcast.7), custom_call_target="tpu_custom_call" | custom-call | tf_op jit(solution)/shard_map/pallas_call | solution.py:487
